TPU v7x, 256 devices: a whole 4x4x8 slice. The times are simulated.
256 devices in a mesh: dp: 16 (over x, y_hi, core), expert: 16 (over z, y_lo).
Axes of the slice: x: 4, y: 4 (y_hi: 2, y_lo: 2; y = y_hi * 2 + y_lo), z: 8, core: 2. Of those that a mesh axis runs over, the one named last changes fastest.
Arguments:
- tokens: bfloat16 [2048, 4096], P('expert', 'dp'), may hold values from -6 to 6
- expert_ids: int32 [2048, 8], P('expert'), may hold values from 0 to 63, all different within a row; in each aligned block of 128 rows (0 to 127, 128 to 255, ...) at most 32 rows name the same one
- gate_prob: float32 [2048, 8], P('expert'), may hold values from 0.05 to 0.35
- w_gate: bfloat16 [64, 4096, 768], P('expert', 'dp'), may hold values from -0.09375 to 0.09375
- w_up: bfloat16 [64, 4096, 768], P('expert', 'dp'), may hold values from -0.09375 to 0.09375
- w_down: bfloat16 [64, 768, 4096], P('expert', None, 'dp'), may hold values from -0.21875 to 0.21875
- grad_out: bfloat16 [2048, 4096], P('expert', 'dp'), may hold values from -6 to 6
Outputs:
- mixed: bfloat16 [2048, 4096], P('expert', 'dp')
- grad_tokens: bfloat16 [2048, 4096], P('expert', 'dp')
- grad_gate: float32 [2048, 8], P('expert')
- grad_w_gate: bfloat16 [64, 4096, 768], P('expert', 'dp')
- grad_w_up: bfloat16 [64, 4096, 768], P('expert', 'dp')
- grad_w_down: bfloat16 [64, 768, 4096], P('expert', None, 'dp')
Inputs may be any that keep to these rules, and one draw needn't show every extreme that they name: `expert_ids`: each row names 8 different experts. Within the rows of one index of expert (aligned blocks of 128 rows) no expert is named by more than 32 rows, a bound that some block reaches.
All inputs are finite; a program needn't handle non-finite values.
Results may differ from a plain program's by a relative error of at most 0.035.
Values may be sent and summed in bfloat16 or wider, within the bound.
No kernel may reach another device: no remote copies, remote signals or barrier semaphores. Data moves between devices by JAX's collectives and lax.ppermute only.
A program may use at most 128 MiB of HBM per device.

v0:
```python
import jax
import jax.numpy as jnp
from jax import lax
from jax.sharding import PartitionSpec as P


def slot_tables(expert_ids, columns, per_device, capacity):
    flat_ids = expert_ids.reshape(-1)
    assign_count = flat_ids.shape[0]
    experts_all = columns * per_device
    onehot = (flat_ids[:, None] == jnp.arange(experts_all, dtype=jnp.int32)[None, :]).astype(
        jnp.int32
    )
    before = jnp.cumsum(onehot, axis=0) - onehot
    rank_in = jnp.sum(before * onehot, axis=1)
    slot_of = (flat_ids % per_device * columns + flat_ids // per_device) * capacity + rank_in
    slot_count = experts_all * capacity
    source = (
        jnp.full((slot_count,), assign_count, jnp.int32)
        .at[slot_of]
        .set(jnp.arange(assign_count, dtype=jnp.int32))
    )
    return (slot_of, source)


def run_groups(bundles, hidden_units):
    parties = lax.axis_size("dp")
    row_totals = [bundle[0].shape[0] * bundle[0].shape[1] for bundle in bundles]
    gate_part = jnp.concatenate(
        [
            jnp.einsum(
                "grd,gdf->grf", bundle[0], bundle[2], preferred_element_type=jnp.float32
            ).reshape(-1, hidden_units)
            for bundle in bundles
        ],
        axis=0,
    )
    up_part = jnp.concatenate(
        [
            jnp.einsum(
                "grd,gdf->grf", bundle[0], bundle[3], preferred_element_type=jnp.float32
            ).reshape(-1, hidden_units)
            for bundle in bundles
        ],
        axis=0,
    )
    total_rows = gate_part.shape[0]
    share_rows = total_rows // parties
    share_start = lax.axis_index("dp") * share_rows
    gate_pre, up_pre = (
        lax.psum(gate_part.astype(jnp.bfloat16), "dp").astype(jnp.float32),
        lax.psum(up_part.astype(jnp.bfloat16), "dp").astype(jnp.float32),
    )
    hidden = (jax.nn.silu(gate_pre) * up_pre).astype(jnp.bfloat16)
    gate_share = lax.dynamic_slice_in_dim(gate_pre, share_start, share_rows, 0)
    up_share = lax.dynamic_slice_in_dim(up_pre, share_start, share_rows, 0)
    hidden_part = jnp.concatenate(
        [
            jnp.einsum(
                "grd,gfd->grf", bundle[1], bundle[4], preferred_element_type=jnp.float32
            ).reshape(-1, hidden_units)
            for bundle in bundles
        ],
        axis=0,
    )
    hidden_grad = lax.psum_scatter(
        hidden_part.astype(jnp.bfloat16), "dp", scatter_dimension=0, tiled=True
    ).astype(jnp.float32)
    sigmoid_g = jax.nn.sigmoid(gate_share)
    gate_grad = (
        hidden_grad * up_share * sigmoid_g * (1.0 + gate_share * (1.0 - sigmoid_g))
    ).astype(jnp.bfloat16)
    up_grad = (hidden_grad * gate_share * sigmoid_g).astype(jnp.bfloat16)
    gate_rows, up_rows = (
        lax.all_gather(gate_grad, "dp", axis=0, tiled=True),
        lax.all_gather(up_grad, "dp", axis=0, tiled=True),
    )
    outputs = []
    offset = 0
    for bundle, row_total in zip(bundles, row_totals):
        piece_shape = (bundle[0].shape[0], bundle[0].shape[1], hidden_units)
        hidden_piece = hidden.reshape(piece_shape)
        gate_piece = gate_rows.reshape(piece_shape)
        up_piece = up_rows.reshape(piece_shape)
        offset = offset + row_total
        expert_out = jnp.einsum(
            "grf,gfd->grd", hidden_piece, bundle[4], preferred_element_type=jnp.float32
        ).astype(jnp.bfloat16)
        slot_grad = (
            jnp.einsum("grf,gdf->grd", gate_piece, bundle[2], preferred_element_type=jnp.float32)
            + jnp.einsum("grf,gdf->grd", up_piece, bundle[3], preferred_element_type=jnp.float32)
        ).astype(jnp.bfloat16)
        dw_gate = jnp.einsum(
            "grd,grf->gdf", bundle[0], gate_piece, preferred_element_type=jnp.float32
        )
        dw_up = jnp.einsum("grd,grf->gdf", bundle[0], up_piece, preferred_element_type=jnp.float32)
        dw_down = jnp.einsum(
            "grf,grd->gfd", hidden_piece, bundle[1], preferred_element_type=jnp.float32
        )
        outputs.append((expert_out, slot_grad, dw_gate, dw_up, dw_down))
    return outputs


def on_device(tokens, expert_ids, gate_prob, w_gate, w_up, w_down, grad_out):
    tok_rows, fanout = expert_ids.shape
    per_device, slice_width, hidden_units = w_gate.shape
    columns = lax.axis_size("expert")
    capacity = 2 * tok_rows * fanout // (per_device * columns)
    slot_count = per_device * columns * capacity
    assign_count = tok_rows * fanout
    slot_of, source = slot_tables(expert_ids, columns, per_device, capacity)
    filled = source < assign_count
    safe_src = jnp.minimum(source, assign_count - 1)
    tok_index = safe_src // fanout
    gate_flat = gate_prob.reshape(-1)
    token_buffer = jnp.where(filled[:, None], tokens[tok_index], jnp.zeros((), jnp.bfloat16))
    gate_slots = jnp.where(filled, gate_flat[safe_src], jnp.zeros((), jnp.float32))
    grad_buffer = (gate_slots[:, None] * grad_out[tok_index].astype(jnp.float32)).astype(
        jnp.bfloat16
    )
    layout = (per_device, columns, capacity, slice_width)
    sent_tokens, sent_grads = (
        lax.all_to_all(
            token_buffer.reshape(layout), "expert", split_axis=1, concat_axis=1, tiled=True
        ),
        lax.all_to_all(
            grad_buffer.reshape(layout), "expert", split_axis=1, concat_axis=1, tiled=True
        ),
    )
    bundles = [
        (
            sent_tokens.reshape(per_device, columns * capacity, slice_width),
            sent_grads.reshape(per_device, columns * capacity, slice_width),
            w_gate,
            w_up,
            w_down,
        )
    ]
    results = run_groups(bundles, hidden_units)
    expert_out = results[0][0].reshape(layout)
    slot_grad = results[0][1].reshape(layout)
    total_gate = results[0][2]
    total_up = results[0][3]
    total_down = results[0][4]
    grad_w_gate = total_gate.astype(jnp.bfloat16)
    grad_w_up = total_up.astype(jnp.bfloat16)
    grad_w_down = total_down.astype(jnp.bfloat16)
    back_out, back_grad = (
        lax.all_to_all(expert_out, "expert", split_axis=1, concat_axis=1, tiled=True),
        lax.all_to_all(slot_grad, "expert", split_axis=1, concat_axis=1, tiled=True),
    )
    out_rows = (
        back_out.reshape(slot_count, slice_width)[slot_of]
        .reshape(tok_rows, fanout, slice_width)
        .astype(jnp.float32)
    )
    grad_rows = (
        back_grad.reshape(slot_count, slice_width)[slot_of]
        .reshape(tok_rows, fanout, slice_width)
        .astype(jnp.float32)
    )
    mixed = jnp.sum(gate_prob[:, :, None] * out_rows, axis=1).astype(jnp.bfloat16)
    grad_tokens = jnp.sum(grad_rows, axis=1).astype(jnp.bfloat16)
    partial_dots = jnp.sum(out_rows * grad_out.astype(jnp.float32)[:, None, :], axis=2)
    grad_gate = lax.psum(partial_dots, "dp")
    return (mixed, grad_tokens, grad_gate, grad_w_gate, grad_w_up, grad_w_down)


def solution(mesh):
    return jax.shard_map(
        on_device,
        mesh=mesh,
        in_specs=(
            P("expert", "dp"),
            P("expert", None),
            P("expert", None),
            P("expert", "dp", None),
            P("expert", "dp", None),
            P("expert", None, "dp"),
            P("expert", "dp"),
        ),
        out_specs=(
            P("expert", "dp"),
            P("expert", "dp"),
            P("expert", None),
            P("expert", "dp", None),
            P("expert", "dp", None),
            P("expert", None, "dp"),
        ),
        check_vma=False,
    )
```

profile of v0, /device:TPU:8, one launch (start us, length us, event | category | flops | bytes accessed | tf_op | source)
XLA Modules:
  0.0 592.3 jit_solution(16468973395299543634)
XLA Ops:
  7.2 0.0 copy-start
  7.2 0.0 all-reduce.3.cloned.1.call-start
  7.2 0.9 copy.47
  8.1 0.1 eq.31
  8.2 0.1 eq.27
  8.3 0.1 reshape.224
  8.4 0.8 copy.46
  9.2 0.1 reshape.230
  9.3 18.0 %reduce-window.6 = s32[64,8,128]{2,1,0:T(8,128)S(1)} reduce-window(s32[64,8,128]{2,1,0:T(8,128)S(1)} %fusion.11, s32[]{:T(128)} %constant.58.clone.1), window={size=1x1x128 pad=0_0x0_0x127_0}, to_apply=%region_0.0 | reduce-window | flops 8323072 | bytes 524292 | tf_op jit(solution)/shard_map/reduce-window
  27.3 0.1 slice.18
  27.5 0.1 copy.50
  27.6 0.1 copy.51
  27.7 0.1 broadcast_add_fusion
  27.9 0.1 fusion.10
  28.0 4.3 scatter_custom_fusion
  32.4 8.6 %gather_fusion.2 = f32[2048]{0:T(1024)S(1)} fusion(f32[1024]{0:T(1024)S(1)} %reshape.230, s32[2048]{0:T(1024)S(1)} %get-tuple-element.26), kind=kCustom, calls=%fused_computation.2 | custom fusion | bytes 24576 | tf_op jit(solution)/shard_map/gather | solution.py:117
  41.0 0.1 broadcast_in_dim.33
  41.1 7.5 %gather_fusion = bf16[2048,256]{1,0:T(8,128)(2,1)S(1)} fusion(bf16[128,256]{1,0:T(8,128)(2,1)S(1)} %copy-done.2, s32[2048]{0:T(1024)S(1)} %get-tuple-element.27), kind=kCustom, calls=%fused_computation | custom fusion | bytes 2105344 | tf_op jit(solution)/shard_map/gather | solution.py:116
  48.6 0.4 copy_select_fusion
  49.1 36.3 %all_to_all.20 = bf16[4,16,32,256]{3,2,0,1:T(8,128)(2,1)S(1)} all-to-all(bf16[4,16,32,256]{3,2,0,1:T(8,128)(2,1)S(1)} %copy_select_fusion), channel_id=1, replica_groups=mesh['dp'=16,'expert'=16] {'expert'}, dimensions={1} | all-to-all | bytes 2097152 | tf_op jit(solution)/shard_map/all_to_all | solution.py:123
  85.4 0.1 copy.54
  85.5 2.6 convolution_convert_fusion.1
  88.1 2.6 convolution_convert_fusion.2
  90.8 0.0 all-reduce.3.cloned.1.call-update
  90.8 0.0 reduce-scatter.2.cloned.1.call-start
  90.9 0.1 mul.97
  91.0 0.7 copy-done.1
  91.6 7.5 %gather_fusion.3 = bf16[2048,256]{1,0:T(8,128)(2,1)S(1)} fusion(bf16[128,256]{1,0:T(8,128)(2,1)S(1)} %copy-done.1, s32[2048]{0:T(1024)S(1)} %get-tuple-element.27), kind=kCustom, calls=%fused_computation.3 | custom fusion | bytes 2105344 | tf_op jit(solution)/shard_map/gather | solution.py:118
  99.1 0.3 fusion
  99.5 32.3 %all_to_all.21 = bf16[4,16,32,256]{3,2,0,1:T(8,128)(2,1)S(1)} all-to-all(bf16[4,16,32,256]{3,2,0,1:T(8,128)(2,1)S(1)} %fusion), channel_id=1, replica_groups=mesh['dp'=16,'expert'=16] {'expert'}, dimensions={1} | all-to-all | bytes 2097152 | tf_op jit(solution)/shard_map/all_to_all | solution.py:126
  131.8 0.1 copy.60
  131.9 2.7 convolution_convert_fusion
  134.6 0.0 reduce-scatter.2.cloned.1.call-update
  134.6 0.0 all-gather.3.cloned.1.call-start
  134.7 137.7 %all-reduce.3.cloned.1.call-done = (bf16[2048,768]{1,0:T(8,128)(2,1)}, bf16[2048,768]{1,0:T(8,128)(2,1)}) async-done(((bf16[2048,768]{1,0:T(8,128)(2,1)}, bf16[2048,768]{1,0:T(8,128)(2,1)}), (bf16[2048,768]{1,0:T(8,128)(2,1)}, bf16[2048,768]{1,0:T(8,128)(2,1)})) %all-reduce.3.cloned.1.call-update) | async-done | bytes 6291472 | tf_op jit(solution)/shard_map/psum | solution.py:52
  272.4 5.2 convert_element_type.91
  277.5 3.1 convert_element_type.94
  280.7 80.2 %reduce-scatter.2.cloned.1.call-done = bf16[128,768]{1,0:T(8,128)(2,1)} async-done(((bf16[2048,768]{1,0:T(8,128)(2,1)}), bf16[128,768]{1,0:T(8,128)(2,1)}) %reduce-scatter.2.cloned.1.call-update) | async-done | bytes 196624 | tf_op jit(solution)/shard_map/reduce_scatter | solution.py:66
  360.8 2.1 fusion.7
  363.0 0.0 all-gather.3.cloned.1.call-update
  363.0 0.0 all-gather.5.cloned.1.call-start
  363.1 0.5 all-gather.5.cloned.1.call-update
  363.6 3.8 multiply_convert_fusion
  367.4 1.0 convolution_convert_fusion.6
  368.4 0.7 copy-done.7
  369.1 1.0 copy.55
  370.2 8.5 %all-to-all-start.1 = ((bf16[4,16,32,256]{3,2,0,1:T(8,128)(2,1)}), bf16[4,16,32,256]{3,2,0,1:T(8,128)(2,1)}, u32[]{:S(2)}, u32[]{:S(2)}) async-start(bf16[4,16,32,256]{3,2,0,1:T(8,128)(2,1)} %copy.55), calls=%async_computation.1 | async-start | bytes 2097152 | tf_op jit(solution)/shard_map/all_to_all | solution.py:149
  378.7 42.4 %all-gather.3.cloned.1.call-done = bf16[2048,768]{1,0:T(8,128)(2,1)} async-done(((bf16[128,768]{1,0:T(8,128)(2,1)}), bf16[2048,768]{1,0:T(8,128)(2,1)}) %all-gather.3.cloned.1.call-update) | async-done | bytes 3145744 | tf_op jit(solution)/shard_map/all_gather | solution.py:75
  421.1 4.7 fusion.20
  425.7 54.1 %all-gather.5.cloned.1.call-done = bf16[2048,768]{1,0:T(8,128)(2,1)} async-done(((bf16[128,768]{1,0:T(8,128)(2,1)}), bf16[2048,768]{1,0:T(8,128)(2,1)}) %all-gather.5.cloned.1.call-update) | async-done | bytes 3145744 | tf_op jit(solution)/shard_map/all_gather | solution.py:76
  479.8 4.0 add_convert_fusion
  483.9 1.1 copy.61
  485.0 8.5 %all-to-all-start.3 = ((bf16[4,16,32,256]{3,2,0,1:T(8,128)(2,1)}), bf16[4,16,32,256]{3,2,0,1:T(8,128)(2,1)}, u32[]{:S(2)}, u32[]{:S(2)}) async-start(bf16[4,16,32,256]{3,2,0,1:T(8,128)(2,1)} %copy.61), calls=%async_computation.4 | async-start | bytes 2097152 | tf_op jit(solution)/shard_map/all_to_all | solution.py:150
  493.5 4.3 convolution_convert_fusion.3
  497.8 1.3 copy.56
  499.1 3.9 gather_fusion.1
  503.0 1.1 fusion.2
  504.2 67.9 %psum.23 = f32[128,8]{1,0:T(8,128)S(1)} all-reduce(f32[128,8]{1,0:T(8,128)S(1)} %get-tuple-element.18), channel_id=1, replica_groups=mesh['dp'=16,'expert'=16] {'dp'}, use_global_device_ids=true, to_apply=%region_10.11 | all-reduce | flops 1024 | bytes 8192 | tf_op jit(solution)/shard_map/psum | solution.py:165
  572.1 0.7 copy.66
  572.8 4.5 convolution_convert_fusion.5
  577.3 2.2 convolution_convert_fusion.4
  579.5 1.3 copy.62
  580.8 3.9 gather_fusion.4
  584.7 1.0 bitcast_reduce_fusion
  (30 shorter events, 0.2 us)
Async XLA Ops:
  7.2 124.7 %copy-start = (bf16[4,768,256]{2,1,0:T(8,128)(2,1)S(1)}, bf16[4,768,256]{2,1,0:T(8,128)(2,1)}, u32[]{:S(2)}) copy-start(bf16[4,768,256]{2,1,0:T(8,128)(2,1)} %param.12) | copy-start | bytes 4718596
  7.2 265.2 %all-reduce.3.cloned.1.call-start = ((), (), s32[]{:S(2)}) async-start(), calls=%async_computation.8 | async-start | bytes 12582912 | tf_op jit(solution)/shard_map/psum | solution.py:52
  32.4 8.7 %copy-start.2 = (bf16[128,256]{1,0:T(8,128)(2,1)S(1)}, bf16[128,256]{1,0:T(8,128)(2,1)}, u32[]{:S(2)}) copy-start(bf16[128,256]{1,0:T(8,128)(2,1)} %param.7) | copy-start | bytes 196612
  48.6 36.9 %copy-start.9 = (bf16[4,256,768]{2,1,0:T(8,128)(2,1)S(1)}, bf16[4,256,768]{2,1,0:T(8,128)(2,1)}, u32[]{:S(2)}) copy-start(bf16[4,256,768]{2,1,0:T(8,128)(2,1)} %param.11) | copy-start | bytes 4718596
  85.5 5.3 copy-start.3
  85.5 2.7 copy-start.8
  90.8 0.8 copy-start.1
  90.8 270.0 %reduce-scatter.2.cloned.1.call-start = ((), (), s32[]{:S(2)}) async-start(), calls=%async_computation.5 | async-start | bytes 3342336 | tf_op jit(solution)/shard_map/reduce_scatter | solution.py:66
  134.6 286.4 %all-gather.3.cloned.1.call-start = ((), (), s32[]{:S(2)}) async-start(), calls=%async_computation.6 | async-start | bytes 3342336 | tf_op jit(solution)/shard_map/all_gather | solution.py:75
  272.4 5.2 copy-start.5
  363.0 116.8 %all-gather.5.cloned.1.call-start = ((), (), s32[]{:S(2)}) async-start(), calls=%async_computation.7 | async-start | bytes 3342336 | tf_op jit(solution)/shard_map/all_gather | solution.py:76
  367.4 1.7 copy-start.7
  370.2 114.8 %all-to-all-start.1 = ((bf16[4,16,32,256]{3,2,0,1:T(8,128)(2,1)}), bf16[4,16,32,256]{3,2,0,1:T(8,128)(2,1)}, u32[]{:S(2)}, u32[]{:S(2)}) async-start(bf16[4,16,32,256]{3,2,0,1:T(8,128)(2,1)} %copy.55), calls=%async_computation.1 | async-start | bytes 2097152 | tf_op jit(solution)/shard_map/all_to_all | solution.py:149
  485.0 94.5 %all-to-all-start.3 = ((bf16[4,16,32,256]{3,2,0,1:T(8,128)(2,1)}), bf16[4,16,32,256]{3,2,0,1:T(8,128)(2,1)}, u32[]{:S(2)}, u32[]{:S(2)}) async-start(bf16[4,16,32,256]{3,2,0,1:T(8,128)(2,1)} %copy.61), calls=%async_computation.4 | async-start | bytes 2097152 | tf_op jit(solution)/shard_map/all_to_all | solution.py:150
  504.2 73.1 %copy-start.4 = (bf16[4,16,32,256]{3,2,1,0:T(8,128)(2,1)S(1)}, bf16[4,16,32,256]{3,2,1,0:T(8,128)(2,1)}, u32[]{:S(2)}) copy-start(bf16[4,16,32,256]{3,2,1,0:T(8,128)(2,1)} %copy-done.3) | copy-start | bytes 3145732
  572.7 4.5 copy-start.6
Sparse Core Ops, SparseCore 0:
  90.9 181.3 all-reduce.2
  276.7 84.1 reduce-scatter.1
  363.5 57.4 all-gather.2
  424.2 55.6 all-gather.4
where the time goes:
time: 594 us; the launch traced here: 592 us
  waiting for transfers between devices  315 us (53%)
  blocking collectives  137 us (23%)
  local copies, waits for them, and re-layouts  45.3 us (8%)
  other arithmetic  35.5 us (6%)
  matrix products  28.7 us (5%)
  starting transfers between devices  17.1 us (3%)
  between operations  14.1 us (2%)
    psum x1, waiting for transfers between devices, run_groups(): lax.psum(up_part.astype(jnp.bfloat16), 'dp').astype(jnp.float32)  138 us
    reduce_scatter x1, waiting for transfers between devices, run_groups(): lax.psum_scatter(hidden_part.astype(jnp.bfloat16), 'dp', scatter_dimensio...  80.2 us
    psum x1, blocking collectives, on_device(): grad_gate = lax.psum(partial_dots, 'dp')  67.9 us
    all_gather x1, waiting for transfers between devices, run_groups(): lax.all_gather(up_grad, 'dp', axis=0, tiled=True)  54.1 us
    all_gather x1, waiting for transfers between devices, run_groups(): lax.all_gather(gate_grad, 'dp', axis=0, tiled=True)  42.4 us
    all_to_all x1, blocking collectives, on_device(): lax.all_to_all(token_buffer.reshape(layout), 'expert', split_axis=1, conc...  36.3 us
    all_to_all x1, blocking collectives, on_device(): lax.all_to_all(grad_buffer.reshape(layout), 'expert', split_axis=1, conca...  32.3 us
    another operation x3, other arithmetic  18.2 us
  transfers between devices with their start and end apart: 6, of which 4 were waited for; matrix products, arithmetic and copies ran while one was open for 9% of the time, Pallas kernels for 0%

commit v1 on v0

v1 whole, which is shorter than its diff:
```python
import jax
import jax.numpy as jnp
from jax import lax
from jax.experimental import pallas as pl
from jax.experimental.pallas import tpu as pltpu
from jax.sharding import PartitionSpec as P

CONTRACT_LAST = (((1,), (1,)), ((), ()))


def gate_up_kernel(own_ref, other_ref, w_own_ref, w_other_ref, out_ref):
    rows = own_ref.shape[0] * own_ref.shape[2]
    own = own_ref[...].reshape(rows, own_ref.shape[3])
    other = other_ref[...].reshape(rows, other_ref.shape[3])
    total = jnp.dot(own, w_own_ref[0], preferred_element_type=jnp.float32)
    total = total + jnp.dot(other, w_other_ref[0], preferred_element_type=jnp.float32)
    out_ref[...] = total.astype(out_ref.dtype).reshape(out_ref.shape)


def gate_up_partials(own, other, w_own, w_other, chips):
    blocks, half, cap, width = own.shape
    wide = w_own.shape[2]
    tile = wide // 2 if wide % 256 == 0 else wide
    rows = blocks * cap
    row_spec = pl.BlockSpec((blocks, 1, cap, width), lambda e, f: (0, e, 0, 0))
    w_spec = pl.BlockSpec((1, width, tile), lambda e, f: (e, 0, f))
    return pl.pallas_call(
        gate_up_kernel,
        out_shape=jax.ShapeDtypeStruct((chips, half, rows // chips, wide), own.dtype),
        grid=(half, wide // tile),
        in_specs=[row_spec, row_spec, w_spec, w_spec],
        out_specs=pl.BlockSpec((chips, 1, rows // chips, tile), lambda e, f: (0, e, 0, f)),
        cost_estimate=pl.CostEstimate(
            flops=4 * half * rows * width * wide,
            bytes_accessed=4 * half * (rows * width + width * wide) + 2 * half * rows * wide,
            transcendentals=0,
        ),
        compiler_params=pltpu.CompilerParams(vmem_limit_bytes=32 * 1024 * 1024),
        name="gate_up_partials",
    )(own, other, w_own, w_other)


def slot_grad_kernel(got_ref, w_own_ref, w_other_ref, own_ref, other_ref):
    wide = w_own_ref.shape[2]
    rows = got_ref.shape[0] * got_ref.shape[2]
    got = got_ref[:, :, :, :wide].reshape(rows, wide)
    for w_ref, out_ref in ((w_other_ref, other_ref), (w_own_ref, own_ref)):
        total = lax.dot_general(got, w_ref[0], CONTRACT_LAST, preferred_element_type=jnp.float32)
        out_ref[0] = total.astype(out_ref.dtype)


def slot_grads(got, w_own, w_other):
    chips, half, share, padded = got.shape
    width, wide = w_own.shape[1:]
    rows = chips * share
    w_spec = pl.BlockSpec((1, width, wide), lambda e: (e, 0, 0))
    out_spec = pl.BlockSpec((1, rows, width), lambda e: (e, 0, 0))
    out = jax.ShapeDtypeStruct((half, rows, width), got.dtype)
    return pl.pallas_call(
        slot_grad_kernel,
        out_shape=(out, out),
        grid=(half,),
        in_specs=[
            pl.BlockSpec((chips, 1, share, padded), lambda e: (0, e, 0, 0)),
            w_spec,
            w_spec,
        ],
        out_specs=(out_spec, out_spec),
        cost_estimate=pl.CostEstimate(
            flops=4 * half * rows * width * wide,
            bytes_accessed=2 * half * rows * padded + 4 * half * (width * wide + rows * width),
            transcendentals=0,
        ),
        compiler_params=pltpu.CompilerParams(vmem_limit_bytes=32 * 1024 * 1024),
        name="slot_grads",
    )(got, w_own, w_other)


def three_pieces(value):
    high = lax.reduce_precision(value, 8, 7)
    rest = value - high
    middle = lax.reduce_precision(rest, 8, 7)
    low = rest - middle
    return [piece.astype(jnp.bfloat16) for piece in (high, middle, low)]


def after(value, earlier):
    return lax.optimization_barrier((value, earlier))[0]


def spread(block, axis_name, size, groups=None):
    copies = jnp.broadcast_to(block[None], (size,) + block.shape)
    return lax.all_to_all(copies, axis_name, 0, 0, tiled=True, axis_index_groups=groups)


def on_device(tokens, expert_ids, gate_prob, w_gate, w_up, w_down, grad_out):
    bf16, f32 = jnp.bfloat16, jnp.float32
    tok, fanout = expert_ids.shape
    n_exp, width, ff = w_gate.shape
    cols = lax.axis_size("expert")
    parties = lax.axis_size("dp")
    cap = 2 * tok * fanout // (n_exp * cols)
    half = n_exp // 2
    chips = parties // 2
    per_share = cols // chips
    share = per_share * cap
    core = lax.axis_index("dp") % 2
    col = lax.axis_index("expert")
    mine, theirs = core * half, (1 - core) * half
    pairs = [(i, i ^ 1) for i in range(parties)]
    same_core = [[i for i in range(parties) if i % 2 == c] for c in (0, 1)]

    levels = cols // 2
    level = col // 2

    def shifted(value, step):
        steps = [(i, (i + 2 * step) % cols) for i in range(cols)]
        return lax.ppermute(value, "expert", steps)

    def swap(value):
        return lax.ppermute(value, "dp", pairs)

    def pick(value, start, axis):
        return lax.dynamic_slice_in_dim(value, start, half, axis)

    with jax.named_scope("send_tokens"):
        routing = jnp.concatenate(
            [expert_ids.T.astype(bf16)] + three_pieces(gate_prob.T), axis=0
        )
        lanes = width // tok
        extra_rows = routing.shape[0] // lanes
        routing = jnp.concatenate(
            [routing[i * extra_rows : (i + 1) * extra_rows] for i in range(lanes)], axis=1
        )
        got_tokens = spread(jnp.concatenate([tokens, routing], axis=0), "expert", cols)
    with jax.named_scope("send_grads"):
        beside = lax.ppermute(grad_out, "expert", [(i, i ^ 1) for i in range(cols)])
        grad_pair = jnp.stack([jnp.where(col % 2 == 0, grad_out, beside), jnp.where(col % 2 == 0, beside, grad_out)])

    with jax.named_scope("swap_weights"):
        w_gate_up = jnp.concatenate([w_gate, w_up], axis=2)
        wgu_mine = pick(w_gate_up, mine, 0)
        wgu_theirs = swap(pick(w_gate_up, theirs, 0))
        wd = jnp.concatenate([pick(w_down, mine, 0), swap(pick(w_down, theirs, 0))], axis=2)

    with jax.named_scope("tables"):
        got_tokens = after(got_tokens, beside)
        all_tokens = got_tokens[:, :tok]
        packed = got_tokens[:, tok:].astype(f32)
        packed = jnp.concatenate([packed[:, :, i * tok : (i + 1) * tok] for i in range(lanes)], axis=1)
        ids = packed[:, :fanout]
        gates = packed[:, fanout : 2 * fanout]
        gates = gates + packed[:, 2 * fanout : 3 * fanout] + packed[:, 3 * fanout :]
        names = (col * n_exp + jnp.arange(n_exp)).astype(f32)
        chosen = ids[:, None] == names[None, :, None, None]
        hit = jnp.sum(chosen.astype(f32), axis=2)
        gate_of = jnp.sum(jnp.where(chosen, gates[:, None], 0.0), axis=2)
        earlier = (jnp.arange(tok)[:, None] < jnp.arange(tok)[None, :]).astype(bf16)
        rank = jnp.einsum("sea,at->set", hit.astype(bf16), earlier, preferred_element_type=f32)
        placed = (rank[:, :, None] == jnp.arange(cap, dtype=f32)[None, None, :, None]) & (
            hit[:, :, None] > 0.5
        )
        slots = placed.astype(bf16)
        gate_slots = jnp.sum(jnp.where(placed, gate_of[:, :, None], 0.0), axis=3)

    def dispatch(source):
        return jnp.einsum(
            "sqt,std->sqd",
            slots.reshape(cols, n_exp * cap, tok),
            source,
            preferred_element_type=f32,
        ).reshape(cols, n_exp, cap, width)

    def join_rows(own, other):
        rows = jnp.concatenate([own, other], axis=3).transpose(1, 0, 2, 3)
        return rows.reshape(half, cols * cap, 2 * width)

    def shares(part):
        return lax.all_to_all(part, "dp", 0, 0, tiled=True, axis_index_groups=same_core)

    def chunks(part):
        part = part.astype(bf16).reshape(half, chips, share, part.shape[-1])
        return part.transpose(1, 0, 2, 3)

    def total(got):
        return jnp.sum(got.astype(f32), axis=0)

    def in_rows(got):
        return got.transpose(1, 0, 2, 3).reshape(half, chips * share, got.shape[-1])

    with jax.named_scope("gate_up"):
        x_all = dispatch(all_tokens).astype(bf16)
        x_mine = pick(x_all, mine, 1)
        x_theirs = swap(pick(x_all, theirs, 1))
        part = gate_up_partials(x_mine, x_theirs, wgu_mine, wgu_theirs, chips)
        x_rows = join_rows(x_mine, x_theirs)
        got_gate_up = shares(part)
        gate_up = total(got_gate_up)
        gate_pre, up_pre = gate_up[..., :ff], gate_up[..., ff:]
        sigmoid_g = jax.nn.sigmoid(gate_pre)
        hidden = (gate_pre * sigmoid_g * up_pre).astype(bf16)
        got_hidden = spread(hidden, "dp", chips, same_core)
        grad_pair = after(grad_pair, part)

    with jax.named_scope("all_grads"):
        all_grads = jnp.zeros((cols, tok, width), bf16)
        for step in range(levels):
            piece = shifted(grad_pair, step) if step else grad_pair
            start = 2 * ((level + levels - step) % levels)
            all_grads = lax.dynamic_update_slice_in_dim(all_grads, piece, start, 0)

    with jax.named_scope("hidden_grad"):
        g_all = (dispatch(all_grads) * gate_slots[..., None]).astype(bf16)
        g_rows = join_rows(pick(g_all, mine, 1), swap(pick(g_all, theirs, 1)))
        part = chunks(jnp.einsum("erd,efd->erf", g_rows, wd, preferred_element_type=f32))
        got = shares(after(part, got_hidden))
        hidden_grad = total(got)
    with jax.named_scope("hidden"):
        all_hidden = in_rows(got_hidden)
    slots_mine = pick(slots, mine, 1)
    slots_theirs = pick(slots, theirs, 1)

    def combine(own, other):
        def part(slot, value):
            return jnp.einsum("sert,esrd->std", slot, value, preferred_element_type=f32)

        shape = (half, cols, cap, width)
        other = swap(other.reshape(shape))
        return (part(slots_mine, own.reshape(shape)) + part(slots_theirs, other)).astype(bf16)

    with jax.named_scope("mixed"):
        expert_out = jnp.einsum("erf,efd->erd", all_hidden, wd, preferred_element_type=f32)
        row_gates = pick(gate_slots, mine, 1).transpose(1, 0, 2).reshape(half, cols * cap)
        out_rows = (expert_out * row_gates[..., None]).astype(bf16)
        mixed_parts = combine(out_rows[..., :width], out_rows[..., width:])
        by_level = mixed_parts.reshape(levels, 2, tok, width)

        def at_level(step):
            return lax.dynamic_index_in_dim(by_level, (level + step) % levels, 0, keepdims=False)

        arrived = [at_level(0)] + [shifted(at_level(step), step) for step in range(1, levels)]
        level_sum = sum(piece.astype(f32) for piece in arrived).astype(bf16)
        even = col % 2 == 0
        keep = jnp.where(even, level_sum[0], level_sum[1])
        give = jnp.where(even, level_sum[1], level_sum[0])
        take = lax.ppermute(give, "expert", [(i, i ^ 1) for i in range(cols)])
        mixed = (keep.astype(f32) + take.astype(f32)).astype(bf16)

    with jax.named_scope("local_grads"):
        gate_grad = (hidden_grad * up_pre * sigmoid_g * (1.0 + gate_pre * (1.0 - sigmoid_g))).astype(bf16)
        up_grad = (hidden_grad * gate_pre * sigmoid_g).astype(bf16)
        my_gates = lax.dynamic_slice_in_dim(
            pick(gate_slots, mine, 1), lax.axis_index("dp") // 2 * per_share, per_share, 0
        ).transpose(1, 0, 2).reshape(half, share)
        dots = jnp.sum(hidden.astype(f32) * hidden_grad, axis=2)
        dots = jnp.where(my_gates > 0, dots / jnp.where(my_gates > 0, my_gates, 1.0), 0.0)
        tail = jnp.stack(three_pieces(dots), axis=-1)
        tail = jnp.pad(tail, ((0, 0), (0, 0), (0, 128 - tail.shape[-1])))
        local_grads = after(jnp.concatenate([gate_grad, up_grad, tail], axis=2), mixed_parts)
        got_grads = spread(local_grads, "dp", chips, same_core)

    with jax.named_scope("grad_tokens"):
        got_grads = after(got_grads, by_level)
        grad_parts = combine(*slot_grads(got_grads, wgu_mine, wgu_theirs))

    with jax.named_scope("grad_gate"):
        all_dots = got_grads[..., 2 * ff : 2 * ff + 3].astype(f32)
        all_dots = (all_dots[..., 0] + all_dots[..., 1] + all_dots[..., 2]).transpose(1, 0, 2)
        all_dots = all_dots.reshape(half, cols, cap)
        their_dots = swap(all_dots)
        first = jnp.where(core == 0, all_dots, their_dots)
        second = jnp.where(core == 0, their_dots, all_dots)
        slot_dots = jnp.concatenate([first, second], axis=0).transpose(1, 0, 2)
        dot_of = jnp.sum(jnp.where(placed, slot_dots[..., None], 0.0), axis=2)
        dot_rows = jnp.concatenate(three_pieces(dot_of), axis=1)
        dot_rows = jnp.pad(dot_rows, ((0, 0), (0, 16 - dot_rows.shape[1]), (0, 0)))
        dot_rows = jnp.concatenate([dot_rows[:, :8], dot_rows[:, 8:]], axis=2)

    with jax.named_scope("return"):
        sent = after(jnp.concatenate([grad_parts, dot_rows], axis=1), mixed)
        back = lax.all_to_all(sent, "expert", 0, 0, tiled=True)
        grad_tokens = jnp.sum(back[:, :tok].astype(f32), axis=0).astype(bf16)
        got_dots = back[:, tok:].astype(f32)
        got_dots = jnp.concatenate([got_dots[..., :tok], got_dots[..., tok:]], axis=1)
        got_dots = (
            got_dots[:, :n_exp] + got_dots[:, n_exp : 2 * n_exp] + got_dots[:, 2 * n_exp : 3 * n_exp]
        ).reshape(cols * n_exp, tok)
        picked = expert_ids.T[:, None] == jnp.arange(cols * n_exp, dtype=expert_ids.dtype)[None, :, None]
        grad_gate = jnp.sum(jnp.where(picked, got_dots[None], 0.0), axis=1).T
        gu_grads = in_rows(after(got_grads, sent)[..., : 2 * ff])

    def both_halves(own, other):
        out = jnp.zeros((n_exp,) + own.shape[1:], own.dtype)
        out = lax.dynamic_update_slice_in_dim(out, own, mine, 0)
        return lax.dynamic_update_slice_in_dim(out, other, theirs, 0)

    with jax.named_scope("weight_grads"):
        dgu = jnp.einsum("erd,erf->edf", x_rows, gu_grads, preferred_element_type=f32).astype(bf16)
        dd = jnp.einsum("erf,erd->efd", all_hidden, g_rows, preferred_element_type=f32).astype(bf16)
        dgu_other = swap(dgu[:, width:])
        dd_other = swap(dd[..., width:])
        grad_w_gate = both_halves(dgu[:, :width, :ff], dgu_other[..., :ff])
        grad_w_up = both_halves(dgu[:, :width, ff:], dgu_other[..., ff:])
        grad_w_down = both_halves(dd[..., :width], dd_other)
    return (mixed, grad_tokens, grad_gate, grad_w_gate, grad_w_up, grad_w_down)


def solution(mesh):
    return jax.shard_map(
        on_device,
        mesh=mesh,
        in_specs=(
            P("expert", "dp"),
            P("expert", None),
            P("expert", None),
            P("expert", "dp", None),
            P("expert", "dp", None),
            P("expert", None, "dp"),
            P("expert", "dp"),
        ),
        out_specs=(
            P("expert", "dp"),
            P("expert", "dp"),
            P("expert", None),
            P("expert", "dp", None),
            P("expert", "dp", None),
            P("expert", None, "dp"),
        ),
        check_vma=False,
    )
```

time: 594 us -> 272 us (0.46)
  waiting for transfers between devices: 315 us -> 136 us
  blocking collectives: 137 us -> 0 us
  starting transfers between devices: 17.1 us -> 61.5 us
  other arithmetic: 35.5 us -> 16.2 us
  matrix products: 28.7 us -> 15.4 us
  between operations: 14.1 us -> 1.47 us
  local copies, waits for them, and re-layouts: 45.3 us -> 34.2 us
    psum x1 -> x0, waiting for transfers between devices: 138 us -> none  [run_groups(): lax.psum(up_part.astype(jnp.bfloat16), 'dp').astype(jnp.float32)]
    all_gather x2 -> x0, waiting for transfers between devices: 96.5 us -> none  [the longest x1 54.1 us: run_groups(): lax.all_gather(up_grad, 'dp', axis=0, tiled=True)]
    all_to_all x2 -> x6, waiting for transfers between devices: 0.01 us -> 86.8 us  [the longest x3 45.3 us: spread(): lax.all_to_all(copies, axis_name, 0, 0, tiled=True, axis_index_groups=gro...]
    reduce_scatter x1 -> x0, waiting for transfers between devices: 80.2 us -> none  [run_groups(): lax.psum_scatter(hidden_part.astype(jnp.bfloat16), 'dp', scatter_dimensio...]
    all_to_all x2 -> x0, blocking collectives: 68.6 us -> none  [the longest x1 36.3 us: on_device(): lax.all_to_all(token_buffer.reshape(layout), 'expert', split_axis=1, conc...]
    psum x1 -> x0, blocking collectives: 67.9 us -> none  [on_device(): grad_gate = lax.psum(partial_dots, 'dp')]
    ppermute x0 -> x25, waiting for transfers between devices: none -> 49.5 us  [the longest x14 30.7 us: shifted(): return lax.ppermute(value, 'expert', steps)]
    gather x5 -> x0, local copies, waits for them, and re-layouts: 31.5 us -> none  [the longest x1 8.58 us: on_device(): gate_flat[safe_src]]
  transfers between devices with their start and end apart: 6 -> 31, of which waited for: 4 -> 21; matrix products, arithmetic and copies ran while one was open for 9% -> 14% of each run, Pallas kernels for 0% -> 1%
where the time goes in v1:
time: 272 us; the launch traced here: 270 us
  waiting for transfers between devices  136 us (50%)
  starting transfers between devices  61.5 us (23%)
  local copies, waits for them, and re-layouts  34.2 us (13%)
  other arithmetic  16.2 us (6%)
  matrix products  15.4 us (6%)
  Pallas kernels  5.19 us (2%)
    all_to_all x3, waiting for transfers between devices, spread(): lax.all_to_all(copies, axis_name, 0, 0, tiled=True, axis_index_groups=gro...  45.3 us
    ppermute x14, waiting for transfers between devices, shifted(): return lax.ppermute(value, 'expert', steps)  30.7 us
    ppermute x14, starting transfers between devices, shifted(): return lax.ppermute(value, 'expert', steps)  24 us
    all_to_all x2, waiting for transfers between devices, shares(): lax.all_to_all(part, 'dp', 0, 0, tiled=True, axis_index_groups=same_core)  23.7 us
    all_to_all x3, starting transfers between devices, spread(): lax.all_to_all(copies, axis_name, 0, 0, tiled=True, axis_index_groups=gro...  18.3 us
    all_to_all x1, waiting for transfers between devices, on_device(): back = lax.all_to_all(sent, 'expert', 0, 0, tiled=True)  17.9 us
    unnamed x52, local copies, waits for them, and re-layouts  11.8 us
    all_to_all x2, starting transfers between devices, shares(): lax.all_to_all(part, 'dp', 0, 0, tiled=True, axis_index_groups=same_core)  9.62 us
  transfers between devices with their start and end apart: 31, of which 21 were waited for; matrix products, arithmetic and copies ran while one was open for 14% of the time, Pallas kernels for 1%

profile of v1, /device:TPU:8, one launch (start us, length us, event | category | flops | bytes accessed | tf_op | source)
XLA Modules:
  0.0 270.3 jit_solution(18248472127800328621)
XLA Ops:
  4.0 9.9 %all-to-all-start = ((bf16[16,144,256]{2,1,0:T(8,128)(2,1)}), bf16[16,144,256]{2,1,0:T(8,128)(2,1)}, u32[]{:S(2)}, u32[]{:S(2)}) async-start(bf16[16,144,256]{2,1,0:T(8,128)(2,1)} %broadcast_in_dim.90), calls=%async_computation | async-start | bytes 2359296 | tf_op jit(solution)/shard_map/send_tokens/all_to_all | solution.py:93
  14.0 1.3 copy-done.13
  15.5 1.4 constant_dynamic-slice_fusion.5
  17.2 4.2 %collective-permute-done = bf16[128,256]{1,0:T(8,128)(2,1)S(1)} collective-permute-done((bf16[128,256]{1,0:T(8,128)(2,1)S(1)}, bf16[128,256]{1,0:T(8,128)(2,1)S(1)}, u32[]{:S(2)}, u32[]{:S(2)}) %collective-permute-start) | collective-permute-done | bytes 65568 | tf_op jit(solution)/shard_map/send_grads/ppermute | solution.py:137
  21.3 22.8 %all-to-all-done = bf16[16,144,256]{2,1,0:T(8,128)(2,1)} async-done(((bf16[16,144,256]{2,1,0:T(8,128)(2,1)}), bf16[16,144,256]{2,1,0:T(8,128)(2,1)}, u32[]{:S(2)}, u32[]{:S(2)}) %all-to-all-start) | async-done | bytes 1179680 | tf_op jit(solution)/shard_map/send_tokens/all_to_all | solution.py:93
  45.8 1.7 convolution_convert_fusion.3
  47.7 1.9 collective-permute-done.1.other_ref
  49.6 2.9 %gate_up_partials.1 = bf16[8,2,64,1536]{3,2,1,0:T(8,128)(2,1)S(1)} custom-call(bf16[16,2,32,256]{3,2,1,0:T(8,128)(2,1)S(1)} %get-tuple-element.50.own_ref, bf16[16,2,32,256]{3,2,1,0:T(8,128)(2,1)S(1)} %collective-permute-done.1.other_ref, bf16[2,256,1536]{2,1,0:T(8,128)(2,1)S(1)} %get-tuple-element.29.w_own_ref, ...), custom_call_target="tpu_custom_call" | custom-call | flops 1610612736 | bytes 7340032 | tf_op jit(solution)/shard_map/gate_up/gate_up_partials/pallas_call | solution.py:27
  52.5 1.6 copy-done.2
  55.7 6.0 %all-to-all-start.1 = ((bf16[8,2,64,1536]{3,2,1,0:T(8,128)(2,1)}), bf16[8,2,64,1536]{3,2,1,0:T(8,128)(2,1)S(1)}, u32[]{:S(2)}, u32[]{:S(2)}) async-start(bf16[8,2,64,1536]{3,2,1,0:T(8,128)(2,1)} %copy-done.2), calls=%async_computation.1 | async-start | bytes 6291456 | tf_op jit(solution)/shard_map/gate_up/all_to_all | solution.py:179
  61.8 2.7 constant_dynamic-slice_fusion.4
  65.9 2.0 collective-permute-start.14
  67.8 2.1 collective-permute-start.15
  69.9 2.8 %collective-permute-start.16 = (bf16[2,128,256]{2,1,0:T(8,128)(2,1)S(1)}, bf16[2,128,256]{2,1,0:T(8,128)(2,1)S(1)}, u32[]{:S(2)}, u32[]{:S(2)}) collective-permute-start(bf16[2,128,256]{2,1,0:T(8,128)(2,1)S(1)} %pad_maximum_fusion.3), channel_id=1, source_target_pairs={{0,8},{1,9},{2,10},{3,11},{4,12},{5,13},{6,14},{7,15},{8,0},{9,1},... | collective-permute-start | bytes 393224 | tf_op jit(solution)/shard_map/all_grads/ppermute | solution.py:118
  72.9 2.3 collective-permute-done.13
  75.2 1.3 collective-permute-done.14
  76.5 1.8 collective-permute-start.18
  78.3 11.3 %collective-permute-done.15 = bf16[2,128,256]{2,1,0:T(8,128)(2,1)S(1)} collective-permute-done((bf16[2,128,256]{2,1,0:T(8,128)(2,1)S(1)}, bf16[2,128,256]{2,1,0:T(8,128)(2,1)S(1)}, u32[]{:S(2)}, u32[]{:S(2)}) %collective-permute-start.15) | collective-permute-done | bytes 131104 | tf_op jit(solution)/shard_map/all_grads/ppermute | solution.py:118
  89.5 2.2 collective-permute-start.19
  91.8 3.4 %collective-permute-done.18 = bf16[2,128,256]{2,1,0:T(8,128)(2,1)S(1)} collective-permute-done((bf16[2,128,256]{2,1,0:T(8,128)(2,1)S(1)}, bf16[2,128,256]{2,1,0:T(8,128)(2,1)S(1)}, u32[]{:S(2)}, u32[]{:S(2)}) %collective-permute-start.18) | collective-permute-done | bytes 131104 | tf_op jit(solution)/shard_map/all_grads/ppermute | solution.py:118
  95.3 2.1 collective-permute-done.19
  97.4 1.8 fusion.48
  99.2 8.3 %all-to-all-done.1 = bf16[8,2,64,1536]{3,2,1,0:T(8,128)(2,1)S(1)} async-done(((bf16[8,2,64,1536]{3,2,1,0:T(8,128)(2,1)}), bf16[8,2,64,1536]{3,2,1,0:T(8,128)(2,1)S(1)}, u32[]{:S(2)}, u32[]{:S(2)}) %all-to-all-start.1) | async-done | bytes 3145760 | tf_op jit(solution)/shard_map/gate_up/all_to_all | solution.py:179
  108.8 1.3 broadcast_in_dim.91
  110.1 4.7 %all-to-all-start.2 = ((bf16[8,2,64,768]{3,2,1,0:T(8,128)(2,1)}), bf16[8,2,64,768]{3,2,1,0:T(8,128)(2,1)}, u32[]{:S(2)}, u32[]{:S(2)}) async-start(bf16[8,2,64,768]{3,2,1,0:T(8,128)(2,1)} %broadcast_in_dim.91), calls=%async_computation.2 | async-start | bytes 3145728 | tf_op jit(solution)/shard_map/gate_up/all_to_all | solution.py:93
  115.5 1.8 collective-permute-done.20
  117.5 1.4 copy-done.21
  118.9 2.1 convolution_convert_fusion.2
  121.0 1.3 copy.105
  122.3 14.8 %all-to-all-done.2 = bf16[8,2,64,768]{3,2,1,0:T(8,128)(2,1)} async-done(((bf16[8,2,64,768]{3,2,1,0:T(8,128)(2,1)}), bf16[8,2,64,768]{3,2,1,0:T(8,128)(2,1)}, u32[]{:S(2)}, u32[]{:S(2)}) %all-to-all-start.2) | async-done | bytes 1572896 | tf_op jit(solution)/shard_map/gate_up/all_to_all | solution.py:93
  137.1 2.7 copy.75
  139.8 3.6 %all-to-all-start.3 = ((bf16[8,2,64,768]{3,2,1,0:T(8,128)(2,1)}), bf16[8,2,64,768]{3,2,1,0:T(8,128)(2,1)S(1)}, u32[]{:S(2)}, u32[]{:S(2)}) async-start(bf16[8,2,64,768]{3,2,1,0:T(8,128)(2,1)} %bitcast.106), calls=%async_computation.3 | async-start | bytes 3145728 | tf_op jit(solution)/shard_map/hidden_grad/all_to_all | solution.py:179
  143.4 2.6 multiply_convert_fusion.1
  148.1 1.6 fusion.1
  149.7 15.3 %all-to-all-done.3 = bf16[8,2,64,768]{3,2,1,0:T(8,128)(2,1)S(1)} async-done(((bf16[8,2,64,768]{3,2,1,0:T(8,128)(2,1)}), bf16[8,2,64,768]{3,2,1,0:T(8,128)(2,1)S(1)}, u32[]{:S(2)}, u32[]{:S(2)}) %all-to-all-start.3) | async-done | bytes 1572896 | tf_op jit(solution)/shard_map/hidden_grad/all_to_all | solution.py:179
  165.7 2.1 broadcast_in_dim.98
  167.8 3.7 %all-to-all-start.4 = ((bf16[8,2,64,1664]{3,2,1,0:T(8,128)(2,1)}), bf16[8,2,64,1664]{3,2,1,0:T(8,128)(2,1)S(1)}, u32[]{:S(2)}, u32[]{:S(2)}) async-start(bf16[8,2,64,1664]{3,2,1,0:T(8,128)(2,1)} %broadcast_in_dim.98), calls=%async_computation.4 | async-start | bytes 6815744 | tf_op jit(solution)/shard_map/local_grads/all_to_all | solution.py:93
  171.5 2.2 dynamic-slice_bitcast_fusion.6
  175.6 1.2 collective-permute-start.5
  176.8 1.8 collective-permute-start.6
  178.6 2.6 collective-permute-start.7
  181.4 2.3 collective-permute-start.8
  183.7 3.3 %collective-permute-start.9 = (bf16[2,128,256]{2,1,0:T(8,128)(2,1)}, bf16[2,128,256]{2,1,0:T(8,128)(2,1)S(1)}, u32[]{:S(2)}, u32[]{:S(2)}) collective-permute-start(bf16[2,128,256]{2,1,0:T(8,128)(2,1)} %get-tuple-element.43), channel_id=1, source_target_pairs={{0,10},{1,11},{2,12},{3,13},{4,14},{5,15},{6,0},{7,1},{8,2},{9,3},... | collective-permute-start | bytes 393224 | tf_op jit(solution)/shard_map/mixed/ppermute | solution.py:118
  187.0 1.3 maximum_bitcast_fusion.1
  189.3 4.6 %collective-permute-done.6 = bf16[2,128,256]{2,1,0:T(8,128)(2,1)S(1)} collective-permute-done((bf16[2,128,256]{2,1,0:T(8,128)(2,1)}, bf16[2,128,256]{2,1,0:T(8,128)(2,1)S(1)}, u32[]{:S(2)}, u32[]{:S(2)}) %collective-permute-start.6) | collective-permute-done | bytes 131104 | tf_op jit(solution)/shard_map/mixed/ppermute | solution.py:118
  194.0 5.4 %collective-permute-done.7 = bf16[2,128,256]{2,1,0:T(8,128)(2,1)S(1)} collective-permute-done((bf16[2,128,256]{2,1,0:T(8,128)(2,1)}, bf16[2,128,256]{2,1,0:T(8,128)(2,1)S(1)}, u32[]{:S(2)}, u32[]{:S(2)}) %collective-permute-start.7) | collective-permute-done | bytes 131104 | tf_op jit(solution)/shard_map/mixed/ppermute | solution.py:118
  199.4 1.2 fusion.23
  200.6 2.0 collective-permute-start.12
  202.6 2.2 convolution_convert_fusion.1
  204.8 6.1 %collective-permute-done.12 = bf16[128,256]{1,0:T(8,128)(2,1)S(1)} collective-permute-done((bf16[128,256]{1,0:T(8,128)(2,1)S(1)}, bf16[128,256]{1,0:T(8,128)(2,1)S(1)}, u32[]{:S(2)}, u32[]{:S(2)}) %collective-permute-start.12) | collective-permute-done | bytes 65568 | tf_op jit(solution)/shard_map/mixed/ppermute | solution.py:246
  211.6 7.6 %all-to-all-done.4.got_ref = bf16[8,2,64,1664]{3,2,1,0:T(8,128)(2,1)S(1)} async-done(((bf16[8,2,64,1664]{3,2,1,0:T(8,128)(2,1)}), bf16[8,2,64,1664]{3,2,1,0:T(8,128)(2,1)S(1)}, u32[]{:S(2)}, u32[]{:S(2)}) %all-to-all-start.4) | async-done | bytes 3407904 | tf_op jit(solution)/shard_map/local_grads/all_to_all | solution.py:93
  219.2 1.1 slice_add_fusion
  220.4 1.2 copy.85
  221.7 1.4 copy-done.1
  223.1 1.4 copy-done.4
  224.5 2.3 slot_grads.1
  230.1 1.1 maximum_maximum_fusion
  231.2 6.0 %all-to-all-start.5 = ((bf16[16,136,256]{2,1,0:T(8,128)(2,1)}), bf16[16,136,256]{2,1,0:T(8,128)(2,1)}, u32[]{:S(2)}, u32[]{:S(2)}) async-start(bf16[16,136,256]{2,1,0:T(8,128)(2,1)} %maximum_maximum_fusion), calls=%async_computation.5 | async-start | bytes 2228224 | tf_op jit(solution)/shard_map/return/all_to_all | solution.py:281
  238.7 1.8 convolution_convert_fusion
  241.0 1.1 copy-done.17
  242.4 2.9 %collective-permute-done.24 = bf16[2,768,256]{2,1,0:T(8,128)(2,1)S(1)} collective-permute-done((bf16[2,768,256]{2,1,0:T(8,128)(2,1)S(1)}, bf16[2,768,256]{2,1,0:T(8,128)(2,1)S(1)}, u32[]{:S(2)}, u32[]{:S(2)}) %collective-permute-start.24) | collective-permute-done | bytes 786464 | tf_op jit(solution)/shard_map/weight_grads/ppermute | solution.py:121
  245.4 1.3 broadcast.106.clone.1
  248.9 17.9 %all-to-all-done.5 = bf16[16,136,256]{2,1,0:T(8,128)(2,1)} async-done(((bf16[16,136,256]{2,1,0:T(8,128)(2,1)}), bf16[16,136,256]{2,1,0:T(8,128)(2,1)}, u32[]{:S(2)}, u32[]{:S(2)}) %all-to-all-start.5) | async-done | bytes 1114144 | tf_op jit(solution)/shard_map/return/all_to_all | solution.py:281
  268.3 2.0 slice_reduce_fusion
  (151 shorter events, 26.8 us)
Async XLA Ops:
  2.9 11.0 %copy-start.12 = (bf16[4,256,768]{2,1,0:T(8,128)(2,1)S(1)}, bf16[4,256,768]{2,1,0:T(8,128)(2,1)}, u32[]{:S(2)}) copy-start(bf16[4,256,768]{2,1,0:T(8,128)(2,1)} %param.10) | copy-start | bytes 4718596
  4.0 40.2 %all-to-all-start = ((bf16[16,144,256]{2,1,0:T(8,128)(2,1)}), bf16[16,144,256]{2,1,0:T(8,128)(2,1)}, u32[]{:S(2)}, u32[]{:S(2)}) async-start(bf16[16,144,256]{2,1,0:T(8,128)(2,1)} %broadcast_in_dim.90), calls=%async_computation | async-start | bytes 2359296 | tf_op jit(solution)/shard_map/send_tokens/all_to_all | solution.py:93
  13.9 1.4 copy-start.13
  15.4 1.4 copy-start.22
  16.8 32.8 %copy-start = (bf16[2,256,1536]{2,1,0:T(8,128)(2,1)}, bf16[2,256,1536]{2,1,0:T(8,128)(2,1)S(1)}, u32[]{:S(2)}) copy-start(bf16[2,256,1536]{2,1,0:T(8,128)(2,1)S(1)} %get-tuple-element.29.w_own_ref) | copy-start | bytes 4718596
  16.8 30.9 %collective-permute-start.2 = (bf16[2,256,1536]{2,1,0:T(8,128)(2,1)}, bf16[2,256,1536]{2,1,0:T(8,128)(2,1)S(1)}, u32[]{:S(2)}, u32[]{:S(2)}) collective-permute-start(bf16[2,256,1536]{2,1,0:T(8,128)(2,1)} %get-tuple-element.28), channel_id=1, source_target_pairs={{0,16},{16,0},{32,48},{48,32},{64,80},{80,64},{96,112},{112,96},{1... | collective-permute-start | bytes 4718600 | tf_op jit(solution)/shard_map/swap_weights/ppermute | solution.py:121
  16.8 4.5 %collective-permute-start = (bf16[128,256]{1,0:T(8,128)(2,1)S(1)}, bf16[128,256]{1,0:T(8,128)(2,1)S(1)}, u32[]{:S(2)}, u32[]{:S(2)}) collective-permute-start(bf16[128,256]{1,0:T(8,128)(2,1)S(1)} %copy-done.22), channel_id=1, source_target_pairs={{0,1},{1,0},{2,3},{3,2},{4,5},{5,4},{6,7},{7,6},{8,9},{9,8},{10,11... | collective-permute-start | bytes 196616 | tf_op jit(solution)/shard_map/send_grads/ppermute | solution.py:137
  21.3 24.0 %copy-start.23 = (bf16[128,256]{1,0:T(8,128)(2,1)}, bf16[128,256]{1,0:T(8,128)(2,1)S(1)}, u32[]{:S(2)}) copy-start(bf16[128,256]{1,0:T(8,128)(2,1)S(1)} %collective-permute-done) | copy-start | bytes 196612
  47.6 2.0 collective-permute-start.1
  47.7 4.8 %copy-start.3 = (bf16[2,256,1536]{2,1,0:T(8,128)(2,1)}, bf16[2,256,1536]{2,1,0:T(8,128)(2,1)S(1)}, u32[]{:S(2)}) copy-start(bf16[2,256,1536]{2,1,0:T(8,128)(2,1)S(1)} %collective-permute-done.2.w_other_ref) | copy-start | bytes 4718596
  52.5 1.6 copy-start.2
  54.1 0.8 copy-start.5
  54.9 0.8 copy-start.6
  55.7 51.8 %all-to-all-start.1 = ((bf16[8,2,64,1536]{3,2,1,0:T(8,128)(2,1)}), bf16[8,2,64,1536]{3,2,1,0:T(8,128)(2,1)S(1)}, u32[]{:S(2)}, u32[]{:S(2)}) async-start(bf16[8,2,64,1536]{3,2,1,0:T(8,128)(2,1)} %copy-done.2), calls=%async_computation.1 | async-start | bytes 6291456 | tf_op jit(solution)/shard_map/gate_up/all_to_all | solution.py:179
  64.4 53.1 %collective-permute-start.3 = (bf16[2,768,256]{2,1,0:T(8,128)(2,1)}, bf16[2,768,256]{2,1,0:T(8,128)(2,1)}, u32[]{:S(2)}, u32[]{:S(2)}) collective-permute-start(bf16[2,768,256]{2,1,0:T(8,128)(2,1)} %get-tuple-element.35), channel_id=1, source_target_pairs={{0,16},{16,0},{32,48},{48,32},{64,80},{80,64},{96,112},{112,96},{1... | collective-permute-start | bytes 2359304 | tf_op jit(solution)/shard_map/swap_weights/ppermute | solution.py:121
  65.3 9.8 %collective-permute-start.13 = (bf16[2,128,256]{2,1,0:T(8,128)(2,1)S(1)}, bf16[2,128,256]{2,1,0:T(8,128)(2,1)S(1)}, u32[]{:S(2)}, u32[]{:S(2)}) collective-permute-start(bf16[2,128,256]{2,1,0:T(8,128)(2,1)S(1)} %pad_maximum_fusion.3), channel_id=1, source_target_pairs={{0,2},{1,3},{2,4},{3,5},{4,6},{5,7},{6,8},{7,9},{8,10},{9,11},{10,... | collective-permute-start | bytes 393224 | tf_op jit(solution)/shard_map/all_grads/ppermute | solution.py:118
  65.9 10.6 %collective-permute-start.14 = (bf16[2,128,256]{2,1,0:T(8,128)(2,1)S(1)}, bf16[2,128,256]{2,1,0:T(8,128)(2,1)S(1)}, u32[]{:S(2)}, u32[]{:S(2)}) collective-permute-start(bf16[2,128,256]{2,1,0:T(8,128)(2,1)S(1)} %pad_maximum_fusion.3), channel_id=1, source_target_pairs={{0,4},{1,5},{2,6},{3,7},{4,8},{5,9},{6,10},{7,11},{8,12},{9,13},{1... | collective-permute-start | bytes 393224 | tf_op jit(solution)/shard_map/all_grads/ppermute | solution.py:118
  67.8 21.7 %collective-permute-start.15 = (bf16[2,128,256]{2,1,0:T(8,128)(2,1)S(1)}, bf16[2,128,256]{2,1,0:T(8,128)(2,1)S(1)}, u32[]{:S(2)}, u32[]{:S(2)}) collective-permute-start(bf16[2,128,256]{2,1,0:T(8,128)(2,1)S(1)} %pad_maximum_fusion.3), channel_id=1, source_target_pairs={{0,6},{1,7},{2,8},{3,9},{4,10},{5,11},{6,12},{7,13},{8,14},{9,15},... | collective-permute-start | bytes 393224 | tf_op jit(solution)/shard_map/all_grads/ppermute | solution.py:118
  69.9 21.8 %collective-permute-start.16 = (bf16[2,128,256]{2,1,0:T(8,128)(2,1)S(1)}, bf16[2,128,256]{2,1,0:T(8,128)(2,1)S(1)}, u32[]{:S(2)}, u32[]{:S(2)}) collective-permute-start(bf16[2,128,256]{2,1,0:T(8,128)(2,1)S(1)} %pad_maximum_fusion.3), channel_id=1, source_target_pairs={{0,8},{1,9},{2,10},{3,11},{4,12},{5,13},{6,14},{7,15},{8,0},{9,1},... | collective-permute-start | bytes 393224 | tf_op jit(solution)/shard_map/all_grads/ppermute | solution.py:118
  75.2 16.6 %collective-permute-start.17 = (bf16[2,128,256]{2,1,0:T(8,128)(2,1)S(1)}, bf16[2,128,256]{2,1,0:T(8,128)(2,1)S(1)}, u32[]{:S(2)}, u32[]{:S(2)}) collective-permute-start(bf16[2,128,256]{2,1,0:T(8,128)(2,1)S(1)} %pad_maximum_fusion.3), channel_id=1, source_target_pairs={{0,10},{1,11},{2,12},{3,13},{4,14},{5,15},{6,0},{7,1},{8,2},{9,3},... | collective-permute-start | bytes 393224 | tf_op jit(solution)/shard_map/all_grads/ppermute | solution.py:118
  76.5 18.8 %collective-permute-start.18 = (bf16[2,128,256]{2,1,0:T(8,128)(2,1)S(1)}, bf16[2,128,256]{2,1,0:T(8,128)(2,1)S(1)}, u32[]{:S(2)}, u32[]{:S(2)}) collective-permute-start(bf16[2,128,256]{2,1,0:T(8,128)(2,1)S(1)} %pad_maximum_fusion.3), channel_id=1, source_target_pairs={{0,12},{1,13},{2,14},{3,15},{4,0},{5,1},{6,2},{7,3},{8,4},{9,5},{1... | collective-permute-start | bytes 393224 | tf_op jit(solution)/shard_map/all_grads/ppermute | solution.py:118
  89.5 7.9 %collective-permute-start.19 = (bf16[2,128,256]{2,1,0:T(8,128)(2,1)S(1)}, bf16[2,128,256]{2,1,0:T(8,128)(2,1)S(1)}, u32[]{:S(2)}, u32[]{:S(2)}) collective-permute-start(bf16[2,128,256]{2,1,0:T(8,128)(2,1)S(1)} %pad_maximum_fusion.3), channel_id=1, source_target_pairs={{0,14},{1,15},{2,0},{3,1},{4,2},{5,3},{6,4},{7,5},{8,6},{9,7},{10,... | collective-permute-start | bytes 393224 | tf_op jit(solution)/shard_map/all_grads/ppermute | solution.py:118
  108.0 0.9 copy-start.8
  110.1 4.7 %copy-start.7 = (f32[16,128,256]{2,1,0:T(8,128)S(1)}, f32[16,128,256]{2,1,0:T(8,128)}, u32[]{:S(2)}) copy-start(f32[16,128,256]{2,1,0:T(8,128)} %fusion.48) | copy-start | bytes 6291460
  110.1 27.0 %all-to-all-start.2 = ((bf16[8,2,64,768]{3,2,1,0:T(8,128)(2,1)}), bf16[8,2,64,768]{3,2,1,0:T(8,128)(2,1)}, u32[]{:S(2)}, u32[]{:S(2)}) async-start(bf16[8,2,64,768]{3,2,1,0:T(8,128)(2,1)} %broadcast_in_dim.91), calls=%async_computation.2 | async-start | bytes 3145728 | tf_op jit(solution)/shard_map/gate_up/all_to_all | solution.py:93
  115.3 2.0 collective-permute-start.20
  117.4 1.5 copy-start.21
  117.5 3.5 %copy-start.18 = (bf16[2,16,32,512]{3,2,1,0:T(8,128)(2,1)}, bf16[2,16,32,512]{3,2,1,0:T(8,128)(2,1)S(1)}, u32[]{:S(2)}) copy-start(bf16[2,16,32,512]{3,2,1,0:T(8,128)(2,1)S(1)} %copy.79) | copy-start | bytes 3145732
  139.8 25.2 %all-to-all-start.3 = ((bf16[8,2,64,768]{3,2,1,0:T(8,128)(2,1)}), bf16[8,2,64,768]{3,2,1,0:T(8,128)(2,1)S(1)}, u32[]{:S(2)}, u32[]{:S(2)}) async-start(bf16[8,2,64,768]{3,2,1,0:T(8,128)(2,1)} %bitcast.106), calls=%async_computation.3 | async-start | bytes 3145728 | tf_op jit(solution)/shard_map/hidden_grad/all_to_all | solution.py:179
  146.1 2.0 collective-permute-start.4
  146.5 1.6 copy-start.10
  149.7 15.6 %copy-start.9 = (f32[2,64,1536]{2,1,0:T(8,128)S(1)}, f32[2,64,1536]{2,1,0:T(8,128)}, u32[]{:S(2)}) copy-start(f32[2,64,1536]{2,1,0:T(8,128)} %copy-done.8) | copy-start | bytes 2359300
  167.8 51.4 %all-to-all-start.4 = ((bf16[8,2,64,1664]{3,2,1,0:T(8,128)(2,1)}), bf16[8,2,64,1664]{3,2,1,0:T(8,128)(2,1)S(1)}, u32[]{:S(2)}, u32[]{:S(2)}) async-start(bf16[8,2,64,1664]{3,2,1,0:T(8,128)(2,1)} %broadcast_in_dim.98), calls=%async_computation.4 | async-start | bytes 6815744 | tf_op jit(solution)/shard_map/local_grads/all_to_all | solution.py:93
  173.7 7.8 %collective-permute-start.10 = (bf16[2,128,256]{2,1,0:T(8,128)(2,1)}, bf16[2,128,256]{2,1,0:T(8,128)(2,1)}, u32[]{:S(2)}, u32[]{:S(2)}) collective-permute-start(bf16[2,128,256]{2,1,0:T(8,128)(2,1)} %get-tuple-element.42), channel_id=1, source_target_pairs={{0,12},{1,13},{2,14},{3,15},{4,0},{5,1},{6,2},{7,3},{8,4},{9,5},{1... | collective-permute-start | bytes 393224 | tf_op jit(solution)/shard_map/mixed/ppermute | solution.py:118
  174.8 9.0 %collective-permute-start.11 = (bf16[2,128,256]{2,1,0:T(8,128)(2,1)}, bf16[2,128,256]{2,1,0:T(8,128)(2,1)}, u32[]{:S(2)}, u32[]{:S(2)}) collective-permute-start(bf16[2,128,256]{2,1,0:T(8,128)(2,1)} %get-tuple-element.41), channel_id=1, source_target_pairs={{0,14},{1,15},{2,0},{3,1},{4,2},{5,3},{6,4},{7,5},{8,6},{9,7},{10,... | collective-permute-start | bytes 393224 | tf_op jit(solution)/shard_map/mixed/ppermute | solution.py:118
  175.6 13.7 %collective-permute-start.5 = (bf16[2,128,256]{2,1,0:T(8,128)(2,1)}, bf16[2,128,256]{2,1,0:T(8,128)(2,1)S(1)}, u32[]{:S(2)}, u32[]{:S(2)}) collective-permute-start(bf16[2,128,256]{2,1,0:T(8,128)(2,1)} %get-tuple-element.40), channel_id=1, source_target_pairs={{0,2},{1,3},{2,4},{3,5},{4,6},{5,7},{6,8},{7,9},{8,10},{9,11},{10,... | collective-permute-start | bytes 393224 | tf_op jit(solution)/shard_map/mixed/ppermute | solution.py:118
  176.8 17.2 %collective-permute-start.6 = (bf16[2,128,256]{2,1,0:T(8,128)(2,1)}, bf16[2,128,256]{2,1,0:T(8,128)(2,1)S(1)}, u32[]{:S(2)}, u32[]{:S(2)}) collective-permute-start(bf16[2,128,256]{2,1,0:T(8,128)(2,1)} %get-tuple-element.46), channel_id=1, source_target_pairs={{0,4},{1,5},{2,6},{3,7},{4,8},{5,9},{6,10},{7,11},{8,12},{9,13},{1... | collective-permute-start | bytes 393224 | tf_op jit(solution)/shard_map/mixed/ppermute | solution.py:118
  178.6 20.7 %collective-permute-start.7 = (bf16[2,128,256]{2,1,0:T(8,128)(2,1)}, bf16[2,128,256]{2,1,0:T(8,128)(2,1)S(1)}, u32[]{:S(2)}, u32[]{:S(2)}) collective-permute-start(bf16[2,128,256]{2,1,0:T(8,128)(2,1)} %get-tuple-element.45), channel_id=1, source_target_pairs={{0,6},{1,7},{2,8},{3,9},{4,10},{5,11},{6,12},{7,13},{8,14},{9,15},... | collective-permute-start | bytes 393224 | tf_op jit(solution)/shard_map/mixed/ppermute | solution.py:118
  181.4 17.9 %collective-permute-start.8 = (bf16[2,128,256]{2,1,0:T(8,128)(2,1)}, bf16[2,128,256]{2,1,0:T(8,128)(2,1)S(1)}, u32[]{:S(2)}, u32[]{:S(2)}) collective-permute-start(bf16[2,128,256]{2,1,0:T(8,128)(2,1)} %get-tuple-element.44), channel_id=1, source_target_pairs={{0,8},{1,9},{2,10},{3,11},{4,12},{5,13},{6,14},{7,15},{8,0},{9,1},... | collective-permute-start | bytes 393224 | tf_op jit(solution)/shard_map/mixed/ppermute | solution.py:118
  183.7 15.7 %collective-permute-start.9 = (bf16[2,128,256]{2,1,0:T(8,128)(2,1)}, bf16[2,128,256]{2,1,0:T(8,128)(2,1)S(1)}, u32[]{:S(2)}, u32[]{:S(2)}) collective-permute-start(bf16[2,128,256]{2,1,0:T(8,128)(2,1)} %get-tuple-element.43), channel_id=1, source_target_pairs={{0,10},{1,11},{2,12},{3,13},{4,14},{5,15},{6,0},{7,1},{8,2},{9,3},... | collective-permute-start | bytes 393224 | tf_op jit(solution)/shard_map/mixed/ppermute | solution.py:118
  188.3 14.3 %copy-start.14 = (bf16[2,8,64,768]{3,2,1,0:T(8,128)(2,1)S(1)}, bf16[2,8,64,768]{3,2,1,0:T(8,128)(2,1)}, u32[]{:S(2)}) copy-start(bf16[2,8,64,768]{3,2,1,0:T(8,128)(2,1)} %copy.75) | copy-start | bytes 4718596
  188.3 14.3 %copy-start.19 = (bf16[2,16,32,512]{3,2,1,0:T(8,128)(2,1)S(1)}, bf16[2,16,32,512]{3,2,1,0:T(8,128)(2,1)}, u32[]{:S(2)}) copy-start(bf16[2,16,32,512]{3,2,1,0:T(8,128)(2,1)} %copy-done.18) | copy-start | bytes 3145732
  200.6 10.3 %collective-permute-start.12 = (bf16[128,256]{1,0:T(8,128)(2,1)S(1)}, bf16[128,256]{1,0:T(8,128)(2,1)S(1)}, u32[]{:S(2)}, u32[]{:S(2)}) collective-permute-start(bf16[128,256]{1,0:T(8,128)(2,1)S(1)} %select_bitcast_fusion.2), channel_id=1, source_target_pairs={{0,1},{1,0},{2,3},{3,2},{4,5},{5,4},{6,7},{7,6},{8,9},{9,8},{10,11... | collective-permute-start | bytes 196616 | tf_op jit(solution)/shard_map/mixed/ppermute | solution.py:246
  221.7 6.3 %collective-permute-start.22 = (f32[2,16,32]{2,1,0:T(8,128)S(1)}, f32[2,16,32]{2,1,0:T(8,128)S(1)}, u32[]{:S(2)}, u32[]{:S(2)}) collective-permute-start(f32[2,16,32]{2,1,0:T(8,128)S(1)} %reshape.173), channel_id=1, source_target_pairs={{0,16},{16,0},{32,48},{48,32},{64,80},{80,64},{96,112},{112,96},{1... | collective-permute-start | bytes 12296 | tf_op jit(solution)/shard_map/grad_gate/ppermute | solution.py:121
  221.7 1.4 copy-start.1
  223.1 1.4 copy-start.4
  224.5 2.3 copy-start.11
  227.4 2.1 collective-permute-start.21
  231.2 35.6 %all-to-all-start.5 = ((bf16[16,136,256]{2,1,0:T(8,128)(2,1)}), bf16[16,136,256]{2,1,0:T(8,128)(2,1)}, u32[]{:S(2)}, u32[]{:S(2)}) async-start(bf16[16,136,256]{2,1,0:T(8,128)(2,1)} %maximum_maximum_fusion), calls=%async_computation.5 | async-start | bytes 2228224 | tf_op jit(solution)/shard_map/return/all_to_all | solution.py:281
  237.5 1.2 copy-start.20
  240.7 1.4 copy-start.17
  240.7 7.1 %collective-permute-start.23 = (bf16[2,256,1536]{2,1,0:T(8,128)(2,1)S(1)}, bf16[2,256,1536]{2,1,0:T(8,128)(2,1)S(1)}, u32[]{:S(2)}, u32[]{:S(2)}) collective-permute-start(bf16[2,256,1536]{2,1,0:T(8,128)(2,1)S(1)} %slice.159), channel_id=1, source_target_pairs={{0,16},{16,0},{32,48},{48,32},{64,80},{80,64},{96,112},{112,96},{1... | collective-permute-start | bytes 4718600 | tf_op jit(solution)/shard_map/weight_grads/ppermute | solution.py:121
  242.2 3.1 %collective-permute-start.24 = (bf16[2,768,256]{2,1,0:T(8,128)(2,1)S(1)}, bf16[2,768,256]{2,1,0:T(8,128)(2,1)S(1)}, u32[]{:S(2)}, u32[]{:S(2)}) collective-permute-start(bf16[2,768,256]{2,1,0:T(8,128)(2,1)S(1)} %get-tuple-element.30), channel_id=1, source_target_pairs={{0,16},{16,0},{32,48},{48,32},{64,80},{80,64},{96,112},{112,96},{1... | collective-permute-start | bytes 2359304 | tf_op jit(solution)/shard_map/weight_grads/ppermute | solution.py:121
  245.4 2.3 copy-start.15
  247.8 19.8 %copy-start.24 = (s32[128,8]{0,1:T(8,128)S(1)}, s32[128,8]{0,1:T(8,128)}, u32[]{:S(2)}) copy-start(s32[128,8]{0,1:T(8,128)} %param.8) | copy-start | bytes 12292
  248.9 21.4 %copy-start.16 = (bf16[4,256,768]{2,1,0:T(8,128)(2,1)}, bf16[4,256,768]{2,1,0:T(8,128)(2,1)S(1)}, u32[]{:S(2)}) copy-start(bf16[4,256,768]{2,1,0:T(8,128)(2,1)S(1)} %get-tuple-element.32) | copy-start | bytes 4718596

commit v2 on v1

v2 whole, which is shorter than its diff:
```python
import functools

import jax
import jax.numpy as jnp
from jax import lax
from jax.experimental import pallas as pl
from jax.experimental.pallas import tpu as pltpu
from jax.sharding import PartitionSpec as P

CONTRACT_LAST = (((1,), (1,)), ((), ()))
CONTRACT_INNER = (((1,), (0,)), ((), ()))


def partials_kernel(contract, own_ref, other_ref, w_own_ref, w_other_ref, out_ref):
    rows = own_ref.shape[0] * own_ref.shape[2]
    own = own_ref[...].reshape(rows, own_ref.shape[3])
    other = other_ref[...].reshape(rows, other_ref.shape[3])
    total = lax.dot_general(own, w_own_ref[0], contract, preferred_element_type=jnp.float32)
    total = total + lax.dot_general(
        other, w_other_ref[0], contract, preferred_element_type=jnp.float32
    )
    out_ref[...] = total.astype(out_ref.dtype).reshape(out_ref.shape)


def partials(own, other, w_own, w_other, chips, width_last):
    blocks, half, cap, width = own.shape
    wide = w_own.shape[1] if width_last else w_own.shape[2]
    tile = wide // 3 if wide % 384 == 0 else wide
    rows = blocks * cap
    row_spec = pl.BlockSpec((blocks, 1, cap, width), lambda e, f: (0, e, 0, 0))
    if width_last:
        w_spec = pl.BlockSpec((1, tile, width), lambda e, f: (e, f, 0))
    else:
        w_spec = pl.BlockSpec((1, width, tile), lambda e, f: (e, 0, f))
    return pl.pallas_call(
        functools.partial(partials_kernel, CONTRACT_LAST if width_last else CONTRACT_INNER),
        out_shape=pltpu.HBM((chips, half, rows // chips, wide), own.dtype),
        grid=(half, wide // tile),
        in_specs=[row_spec, row_spec, w_spec, w_spec],
        out_specs=pl.BlockSpec((chips, 1, rows // chips, tile), lambda e, f: (0, e, 0, f)),
        cost_estimate=pl.CostEstimate(
            flops=4 * half * rows * width * wide,
            bytes_accessed=4 * half * (rows * width + width * wide) + 2 * half * rows * wide,
            transcendentals=0,
        ),
        compiler_params=pltpu.CompilerParams(vmem_limit_bytes=32 * 1024 * 1024),
        name="partials",
    )(own, other, w_own, w_other)


def expert_out_kernel(
    got_ref, gate_ref, g_own_ref, g_other_ref, w_own_ref, w_other_ref, own_ref, other_ref, dots_ref
):
    rows = got_ref.shape[0] * got_ref.shape[2]
    got = got_ref[...].reshape(rows, got_ref.shape[3])
    gates = gate_ref[0]
    dots = jnp.zeros((rows, 1), jnp.float32)
    for w_ref, g_ref, out_ref in (
        (w_other_ref, g_other_ref, other_ref),
        (w_own_ref, g_own_ref, own_ref),
    ):
        total = jnp.dot(got, w_ref[0], preferred_element_type=jnp.float32)
        grads = g_ref[...].reshape(rows, g_ref.shape[3]).astype(jnp.float32)
        dots = dots + jnp.sum(total * grads, axis=1, keepdims=True)
        out_ref[...] = (total * gates).astype(out_ref.dtype).reshape(out_ref.shape)
    filled = gates > 0
    dots_ref[0] = jnp.where(filled, dots / jnp.where(filled, gates, 1.0), 0.0)


def slot_grad_kernel(got_ref, w_own_ref, w_other_ref, own_ref, other_ref):
    rows = got_ref.shape[0] * got_ref.shape[2]
    got = got_ref[...].reshape(rows, got_ref.shape[3])
    for w_ref, out_ref in ((w_other_ref, other_ref), (w_own_ref, own_ref)):
        total = lax.dot_general(got, w_ref[0], CONTRACT_LAST, preferred_element_type=jnp.float32)
        out_ref[...] = total.astype(out_ref.dtype).reshape(out_ref.shape)


def per_expert(kernel, got, w_own, w_other, cap, width_last, gates=None, grads=()):
    chips, half, share, wide = got.shape
    width = w_own.shape[1] if width_last else w_own.shape[2]
    rows = chips * share
    w_spec = pl.BlockSpec((1,) + w_own.shape[1:], lambda e, p: (e, 0, 0))
    row_spec = pl.BlockSpec((rows // cap // 2, 1, cap, width), lambda e, p: (p, e, 0, 0))
    column_spec = pl.BlockSpec((1, rows // 2, 1), lambda e, p: (e, p, 0))
    outs = [jax.ShapeDtypeStruct((rows // cap, half, cap, width), got.dtype)] * 2
    out_specs = [row_spec, row_spec]
    in_specs = [pl.BlockSpec((chips // 2, 1, share, wide), lambda e, p: (p, e, 0, 0))]
    args = [got]
    if gates is not None:
        in_specs = in_specs + [column_spec, row_spec, row_spec]
        args = args + [gates, *grads]
        outs = outs + [jax.ShapeDtypeStruct((half, rows, 1), jnp.float32)]
        out_specs = out_specs + [column_spec]
    return pl.pallas_call(
        kernel,
        out_shape=outs,
        grid=(half, 2),
        in_specs=in_specs + [w_spec, w_spec],
        out_specs=out_specs,
        cost_estimate=pl.CostEstimate(
            flops=4 * half * rows * width * wide,
            bytes_accessed=2 * half * rows * wide + 4 * half * (width * wide + rows * width),
            transcendentals=0,
        ),
        compiler_params=pltpu.CompilerParams(vmem_limit_bytes=32 * 1024 * 1024),
        name=kernel.__name__,
    )(*args, w_own, w_other)


def merge_kernel(odd_ref, *refs):
    pieces, (keep_ref, give_ref) = refs[:-2], refs[-2:]
    extra = (keep_ref.shape[0] - pieces[0].shape[1]) // (len(pieces) - 1)
    tok = pieces[0].shape[1] - extra
    odd = odd_ref[0] == 1

    def store(rows, values):
        keep_ref[rows] = jnp.where(odd, values[1], values[0])
        give_ref[rows] = jnp.where(odd, values[0], values[1])

    total = pieces[0][:, :tok].astype(jnp.float32)
    for piece in pieces[1:]:
        total = total + piece[:, :tok].astype(jnp.float32)
    store(slice(0, tok), total.astype(keep_ref.dtype))
    for index, piece in enumerate(pieces):
        start = tok + index * extra
        store(slice(start, start + extra), piece[:, tok:])


def merge(odd, pieces, extra):
    tok, width = pieces[0].shape[1] - extra, pieces[0].shape[2]
    out = jax.ShapeDtypeStruct((tok + extra * len(pieces), width), pieces[0].dtype)
    vmem = pl.BlockSpec(memory_space=pltpu.VMEM)
    return pl.pallas_call(
        merge_kernel,
        out_shape=(out, out),
        in_specs=[pl.BlockSpec(memory_space=pltpu.SMEM)] + [vmem] * len(pieces),
        out_specs=(vmem, vmem),
        name="merge",
    )(odd.reshape(1), *pieces)


def three_pieces(value):
    high = lax.reduce_precision(value, 8, 7)
    rest = value - high
    middle = lax.reduce_precision(rest, 8, 7)
    low = rest - middle
    return [piece.astype(jnp.bfloat16) for piece in (high, middle, low)]


def after(value, earlier):
    return lax.optimization_barrier((value, earlier))[0]


def spread(block, axis_name, size, groups=None):
    copies = jnp.broadcast_to(block[None], (size,) + block.shape)
    return lax.all_to_all(copies, axis_name, 0, 0, tiled=True, axis_index_groups=groups)


def on_device(tokens, expert_ids, gate_prob, w_gate, w_up, w_down, grad_out):
    bf16, f32 = jnp.bfloat16, jnp.float32
    tok, fanout = expert_ids.shape
    n_exp, width, ff = w_gate.shape
    cols = lax.axis_size("expert")
    parties = lax.axis_size("dp")
    cap = 2 * tok * fanout // (n_exp * cols)
    half = n_exp // 2
    chips = parties // 2
    per_share = cols // chips
    share = per_share * cap
    core = lax.axis_index("dp") % 2
    col = lax.axis_index("expert")
    mine, theirs = core * half, (1 - core) * half
    pairs = [(i, i ^ 1) for i in range(parties)]
    same_core = [[i for i in range(parties) if i % 2 == c] for c in (0, 1)]

    levels = cols // 2
    level = col // 2

    def shifted(value, step):
        steps = [(i, (i + 2 * step) % cols) for i in range(cols)]
        return lax.ppermute(value, "expert", steps)

    def swap(value):
        return lax.ppermute(value, "dp", pairs)

    def pick(value, start, axis):
        return lax.dynamic_slice_in_dim(value, start, half, axis)

    def packed(rows):
        lanes = width // tok
        each = -(-rows.shape[0] // (8 * lanes)) * 8
        rows = jnp.pad(rows, ((0, each * lanes - rows.shape[0]), (0, 0)))
        return jnp.concatenate([rows[i * each : (i + 1) * each] for i in range(lanes)], axis=1)

    def unpacked(rows, count):
        lanes = width // tok
        parts = [rows[:, :, i * tok : (i + 1) * tok] for i in range(lanes)]
        return jnp.concatenate(parts, axis=1)[:, :count].astype(f32)

    with jax.named_scope("send_tokens"):
        routing = packed(expert_ids.T.astype(bf16))
        got_tokens = spread(jnp.concatenate([tokens, routing], axis=0), "expert", cols)
    with jax.named_scope("send_grads"):
        own_grads = jnp.concatenate(
            [grad_out, packed(jnp.concatenate(three_pieces(gate_prob.T), axis=0))], axis=0
        )
        beside = lax.ppermute(own_grads, "expert", [(i, i ^ 1) for i in range(cols)])
        even = col % 2 == 0
        grad_pair = jnp.stack(
            [jnp.where(even, own_grads, beside), jnp.where(even, beside, own_grads)]
        )

    with jax.named_scope("swap_weights"):
        w_gate_up = jnp.concatenate([w_gate, w_up], axis=2)
        wgu_mine = pick(w_gate_up, mine, 0)
        wgu_theirs = swap(pick(w_gate_up, theirs, 0))
        wd_mine = pick(w_down, mine, 0)
        wd_theirs = swap(pick(w_down, theirs, 0))

    with jax.named_scope("tables"):
        got_tokens = after(got_tokens, (beside, wd_theirs))
        all_tokens = got_tokens[:, :tok]
        ids = unpacked(got_tokens[:, tok:], fanout)
        names = (col * n_exp + jnp.arange(n_exp)).astype(f32)
        chosen = ids[:, None] == names[None, :, None, None]
        hit = jnp.sum(chosen.astype(f32), axis=2)
        earlier = (jnp.arange(tok)[:, None] < jnp.arange(tok)[None, :]).astype(bf16)
        rank = jnp.einsum("sea,at->set", hit.astype(bf16), earlier, preferred_element_type=f32)
        placed = (rank[:, :, None] == jnp.arange(cap, dtype=f32)[None, None, :, None]) & (
            hit[:, :, None] > 0.5
        )
        slots = placed.astype(bf16)

    def dispatch(source):
        return jnp.einsum(
            "sqt,std->sqd",
            slots.reshape(cols, n_exp * cap, tok),
            source,
            preferred_element_type=f32,
        ).reshape(cols, n_exp, cap, width)

    def join_rows(own, other):
        rows = jnp.concatenate([own, other], axis=3).transpose(1, 0, 2, 3)
        return rows.reshape(half, cols * cap, 2 * width)

    def shares(part):
        return lax.all_to_all(part, "dp", 0, 0, tiled=True, axis_index_groups=same_core)

    def total(got):
        return jnp.sum(got.astype(f32), axis=0)

    def in_rows(got):
        return got.transpose(1, 0, 2, 3).reshape(half, chips * share, got.shape[-1])

    with jax.named_scope("gate_up"):
        x_all = dispatch(all_tokens).astype(bf16)
        x_mine = pick(x_all, mine, 1)
        x_theirs = swap(pick(x_all, theirs, 1))
        part = partials(x_mine, x_theirs, wgu_mine, wgu_theirs, chips, False)
        got_gate_up = shares(part)
        gate_up = total(got_gate_up)
        gate_pre, up_pre = gate_up[..., :ff], gate_up[..., ff:]
        sigmoid_g = jax.nn.sigmoid(gate_pre)
        hidden = (gate_pre * sigmoid_g * up_pre).astype(bf16)
        got_hidden = spread(hidden, "dp", chips, same_core)
        grad_pair = after(grad_pair, part)

    with jax.named_scope("all_grads"):
        all_grads = jnp.zeros((cols,) + own_grads.shape, bf16)
        for step in range(levels):
            piece = shifted(grad_pair, step) if step else grad_pair
            start = 2 * ((level + levels - step) % levels)
            all_grads = lax.dynamic_update_slice_in_dim(all_grads, piece, start, 0)

    with jax.named_scope("hidden_grad"):
        gates = unpacked(all_grads[:, tok:], 3 * fanout)
        gates = gates[:, :fanout] + gates[:, fanout : 2 * fanout] + gates[:, 2 * fanout :]
        gate_of = jnp.sum(jnp.where(chosen, gates[:, None], 0.0), axis=2)
        gate_slots = jnp.sum(jnp.where(placed, gate_of[:, :, None], 0.0), axis=3)
        g_all = (dispatch(all_grads[:, :tok]) * gate_slots[..., None]).astype(bf16)
        g_mine = pick(g_all, mine, 1)
        g_theirs = swap(pick(g_all, theirs, 1))
        part = partials(g_mine, g_theirs, wd_mine, wd_theirs, chips, True)
        got = shares(after(part, got_hidden))
        hidden_grad = total(got)
    slots_mine = pick(slots, mine, 1).reshape(cols, half * cap, tok)
    slots_theirs = pick(slots, theirs, 1).reshape(cols, half * cap, tok)

    def combine(own, other):
        def part(slot, value):
            value = value.reshape(cols, half * cap, width)
            return jnp.einsum("sqt,sqd->std", slot, value, preferred_element_type=f32)

        return (part(slots_mine, own) + part(slots_theirs, other)).astype(bf16)

    with jax.named_scope("mixed"):
        row_gates = pick(gate_slots, mine, 1).transpose(1, 0, 2).reshape(half, cols * cap, 1)
        out_own, out_other, dots = per_expert(
            expert_out_kernel, got_hidden, wd_mine, wd_theirs, cap, False, row_gates, (g_mine, g_theirs)
        )
        mixed_parts = combine(out_own, swap(out_other))
        slot_dots = dots.reshape(half, cols, cap).transpose(1, 0, 2)
        dot_of = jnp.sum(jnp.where(pick(placed, mine, 1), slot_dots[..., None], 0.0), axis=2)
        dot_rows = jax.vmap(packed)(jnp.concatenate(three_pieces(dot_of), axis=1))
        extra = dot_rows.shape[1]
        outgoing = jnp.concatenate([mixed_parts, dot_rows], axis=1)
        by_level = outgoing.reshape(levels, 2, tok + extra, width)

        def at_level(step):
            return lax.dynamic_index_in_dim(by_level, (level + step) % levels, 0, keepdims=False)

        arrived = [at_level(0)] + [shifted(at_level(step), step) for step in range(1, levels)]
        keep, give = merge((col % 2).astype(jnp.int32), arrived, extra)
        take = lax.ppermute(give, "expert", [(i, i ^ 1) for i in range(cols)])
        mixed = (keep[:tok].astype(f32) + take[:tok].astype(f32)).astype(bf16)

    with jax.named_scope("local_grads"):
        gate_grad = (hidden_grad * up_pre * sigmoid_g * (1.0 + gate_pre * (1.0 - sigmoid_g))).astype(bf16)
        up_grad = (hidden_grad * gate_pre * sigmoid_g).astype(bf16)
        local_grads = after(jnp.concatenate([gate_grad, up_grad], axis=2), outgoing)
        got_grads = spread(local_grads, "dp", chips, same_core)

    with jax.named_scope("grad_tokens"):
        g_rows = join_rows(g_mine, g_theirs)
        all_hidden = in_rows(after(got_hidden, mixed_parts))
        dd = jnp.einsum("erf,erd->efd", all_hidden, g_rows, preferred_element_type=f32).astype(bf16)
        got_grads = after(got_grads, (take, dd))
        slot_own, slot_other = per_expert(
            slot_grad_kernel, got_grads, wgu_mine, wgu_theirs, cap, True
        )
        grad_parts = after(combine(slot_own, swap(slot_other)), mixed)
        back = lax.all_to_all(grad_parts, "expert", 0, 0, tiled=True)
        grad_tokens = jnp.sum(back.astype(f32), axis=0).astype(bf16)
        gu_grads = in_rows(after(got_grads, grad_parts))

    with jax.named_scope("grad_gate"):
        both = jnp.concatenate([keep[tok:], take[tok:]], axis=0)
        both = unpacked(both.reshape(2 * levels, extra, width), 3 * half)
        values = (both[:, :half] + both[:, half : 2 * half] + both[:, 2 * half :]).reshape(-1, tok)
        from_level = (level + levels - jnp.arange(levels)) % levels
        from_col = jnp.concatenate([2 * from_level + col % 2, 2 * from_level + 1 - col % 2])
        owners = (from_col[:, None] * n_exp + mine + jnp.arange(half)[None, :]).reshape(-1)
        picked = expert_ids.T[:, None] == owners[None, :, None].astype(expert_ids.dtype)
        gate_sum = after(jnp.sum(jnp.where(picked, values[None], 0.0), axis=1), grad_parts)
        bit = 1
        while bit < parties:
            gate_sum = gate_sum + lax.ppermute(gate_sum, "dp", [(i, i ^ bit) for i in range(parties)])
            bit = bit * 2
        grad_gate = gate_sum.T

    def both_halves(own, other):
        out = jnp.zeros((n_exp,) + own.shape[1:], own.dtype)
        out = lax.dynamic_update_slice_in_dim(out, own, mine, 0)
        return lax.dynamic_update_slice_in_dim(out, other, theirs, 0)

    with jax.named_scope("weight_grads"):
        x_rows = join_rows(after(x_mine, grad_parts), x_theirs)
        dd = after(dd, grad_parts)
        dgu = jnp.einsum("erd,erf->edf", x_rows, gu_grads, preferred_element_type=f32).astype(bf16)
        dgu_other = swap(dgu[:, width:])
        dd_other = swap(dd[..., width:])
        grad_w_gate = both_halves(dgu[:, :width, :ff], dgu_other[..., :ff])
        grad_w_up = both_halves(dgu[:, :width, ff:], dgu_other[..., ff:])
        grad_w_down = both_halves(dd[..., :width], dd_other)
    return (mixed, grad_tokens, grad_gate, grad_w_gate, grad_w_up, grad_w_down)


def solution(mesh):
    return jax.shard_map(
        on_device,
        mesh=mesh,
        in_specs=(
            P("expert", "dp"),
            P("expert", None),
            P("expert", None),
            P("expert", "dp", None),
            P("expert", "dp", None),
            P("expert", None, "dp"),
            P("expert", "dp"),
        ),
        out_specs=(
            P("expert", "dp"),
            P("expert", "dp"),
            P("expert", None),
            P("expert", "dp", None),
            P("expert", "dp", None),
            P("expert", None, "dp"),
        ),
        check_vma=False,
    )
```

time: 272 us -> 266 us (0.978)
  waiting for transfers between devices: 136 us -> 104 us
  Pallas kernels: 5.19 us -> 22.5 us
  starting transfers between devices: 61.5 us -> 72.9 us
    pallas_call x2 -> x5, Pallas kernels: 5.19 us -> 22.5 us  [the longest x2 11.8 us: partials(): pl.pallas_call(functools.partial(partials_kernel, CONTRACT_LAST if width_...]
    all_to_all x1, waiting for transfers between devices: 17.9 us -> 4.07 us  [on_device(): back = lax.all_to_all(grad_parts, 'expert', 0, 0, tiled=True)]
    ppermute x14, starting transfers between devices: 24 us -> 34.5 us  [shifted(): return lax.ppermute(value, 'expert', steps)]
    ppermute x1 -> x5, waiting for transfers between devices: 4.16 us -> 14.3 us  [the longest x4 13 us: on_device(): lax.ppermute(gate_sum, 'dp', [(i, i ^ bit) for i in range(parties)])]
    all_to_all x3, waiting for transfers between devices: 45.3 us -> 36.3 us  [spread(): lax.all_to_all(copies, axis_name, 0, 0, tiled=True, axis_index_groups=gro...]
    ppermute x1, waiting for transfers between devices: 6.13 us -> 0.01 us  [on_device(): take = lax.ppermute(give, 'expert', [(i, i ^ 1) for i in range(cols)])]
    ppermute x9 -> x8, waiting for transfers between devices: 8.54 us -> 2.78 us  [swap(): return lax.ppermute(value, 'dp', pairs)]
    ppermute x14, waiting for transfers between devices: 30.7 us -> 26.6 us  [shifted(): return lax.ppermute(value, 'expert', steps)]
  transfers between devices with their start and end apart: 31 -> 34, of which waited for: 21 -> 23; matrix products, arithmetic and copies ran while one was open for 14% -> 13% of each run, Pallas kernels for 1% -> 4%
where the time goes in v2:
time: 266 us; the launch traced here: 264 us
  waiting for transfers between devices  104 us (39%)
  starting transfers between devices  72.9 us (27%)
  local copies, waits for them, and re-layouts  32.4 us (12%)
  Pallas kernels  22.5 us (8%)
  other arithmetic  17.7 us (7%)
  matrix products  13.2 us (5%)
    all_to_all x3, waiting for transfers between devices, spread(): lax.all_to_all(copies, axis_name, 0, 0, tiled=True, axis_index_groups=gro...  36.3 us
    ppermute x14, starting transfers between devices, shifted(): return lax.ppermute(value, 'expert', steps)  34.5 us
    ppermute x14, waiting for transfers between devices, shifted(): return lax.ppermute(value, 'expert', steps)  26.6 us
    all_to_all x2, waiting for transfers between devices, shares(): lax.all_to_all(part, 'dp', 0, 0, tiled=True, axis_index_groups=same_core)  20 us
    all_to_all x3, starting transfers between devices, spread(): lax.all_to_all(copies, axis_name, 0, 0, tiled=True, axis_index_groups=gro...  18.1 us
    ppermute x4, waiting for transfers between devices, on_device(): lax.ppermute(gate_sum, 'dp', [(i, i ^ bit) for i in range(parties)])  13 us
    unnamed x82, local copies, waits for them, and re-layouts  12.5 us
    pallas_call x2, Pallas kernels, partials(): pl.pallas_call(functools.partial(partials_kernel, CONTRACT_LAST if width_...  11.8 us
  transfers between devices with their start and end apart: 34, of which 23 were waited for; matrix products, arithmetic and copies ran while one was open for 13% of the time, Pallas kernels for 4%

profile of v2, /device:TPU:8, one launch (start us, length us, event | category | flops | bytes accessed | tf_op | source)
XLA Modules:
  0.0 264.3 jit_solution(16791787645605928572)
XLA Ops:
  3.2 9.9 %all-to-all-start = ((bf16[16,136,256]{2,1,0:T(8,128)(2,1)}), bf16[16,136,256]{2,1,0:T(8,128)(2,1)}, u32[]{:S(2)}, u32[]{:S(2)}) async-start(bf16[16,136,256]{2,1,0:T(8,128)(2,1)} %broadcast_in_dim.88), calls=%async_computation | async-start | bytes 2228224 | tf_op jit(solution)/shard_map/send_tokens/all_to_all | solution.py:156
  15.9 1.4 constant_dynamic-slice_fusion.4
  17.8 1.3 collective-permute-done
  19.0 23.0 %all-to-all-done = bf16[16,136,256]{2,1,0:T(8,128)(2,1)} async-done(((bf16[16,136,256]{2,1,0:T(8,128)(2,1)}), bf16[16,136,256]{2,1,0:T(8,128)(2,1)}, u32[]{:S(2)}, u32[]{:S(2)}) %all-to-all-start) | async-done | bytes 1114144 | tf_op jit(solution)/shard_map/send_tokens/all_to_all | solution.py:156
  43.4 1.7 convolution_convert_fusion.2
  45.3 1.9 collective-permute-done.2.other_ref
  47.2 6.4 %partials.2 = bf16[8,2,64,1536]{3,2,1,0:T(8,128)(2,1)} custom-call(bf16[16,2,32,256]{3,2,1,0:T(8,128)(2,1)S(1)} %get-tuple-element.39.own_ref, bf16[16,2,32,256]{3,2,1,0:T(8,128)(2,1)S(1)} %collective-permute-done.2.other_ref, bf16[2,256,1536]{2,1,0:T(8,128)(2,1)S(1)} %get-tuple-element.45.w_own_ref, bf16[2,256,1536]{2,1,0:T(8,128)(2,1)} %collective-permute-done.3.w_other_ref), custom_call_target="tpu_custom_call" | custom-call | flops 1610612736 | bytes 7340032 | tf_op jit(solution)/shard_map/gate_up/partials/pallas_call | solution.py:35
  53.6 6.2 %all-to-all-start.1 = ((bf16[8,2,64,1536]{3,2,1,0:T(8,128)(2,1)}), bf16[8,2,64,1536]{3,2,1,0:T(8,128)(2,1)}, u32[]{:S(2)}, u32[]{:S(2)}) async-start(bf16[8,2,64,1536]{3,2,1,0:T(8,128)(2,1)} %partials.2), calls=%async_computation.1 | async-start | bytes 6291456 | tf_op jit(solution)/shard_map/gate_up/all_to_all | solution.py:247
  60.1 1.8 collective-permute-start.5
  61.8 2.0 collective-permute-start.6
  63.9 3.0 %collective-permute-start.7 = (bf16[2,144,256]{2,1,0:T(8,128)(2,1)S(1)}, bf16[2,144,256]{2,1,0:T(8,128)(2,1)S(1)}, u32[]{:S(2)}, u32[]{:S(2)}) collective-permute-start(bf16[2,144,256]{2,1,0:T(8,128)(2,1)S(1)} %pad_maximum_fusion.1), channel_id=1, source_target_pairs={{0,8},{1,9},{2,10},{3,11},{4,12},{5,13},{6,14},{7,15},{8,0},{9,1},... | collective-permute-start | bytes 442376 | tf_op jit(solution)/shard_map/all_grads/ppermute | solution.py:181
  66.8 1.8 collective-permute-start.8
  68.7 2.9 %collective-permute-done.4 = bf16[2,144,256]{2,1,0:T(8,128)(2,1)S(1)} collective-permute-done((bf16[2,144,256]{2,1,0:T(8,128)(2,1)S(1)}, bf16[2,144,256]{2,1,0:T(8,128)(2,1)S(1)}, u32[]{:S(2)}, u32[]{:S(2)}) %collective-permute-start.4) | collective-permute-done | bytes 147488 | tf_op jit(solution)/shard_map/all_grads/ppermute | solution.py:181
  72.6 6.7 %collective-permute-start.10 = (bf16[2,144,256]{2,1,0:T(8,128)(2,1)S(1)}, bf16[2,144,256]{2,1,0:T(8,128)(2,1)S(1)}, u32[]{:S(2)}, u32[]{:S(2)}) collective-permute-start(bf16[2,144,256]{2,1,0:T(8,128)(2,1)S(1)} %pad_maximum_fusion.1), channel_id=1, source_target_pairs={{0,14},{1,15},{2,0},{3,1},{4,2},{5,3},{6,4},{7,5},{8,6},{9,7},{10,... | collective-permute-start | bytes 442376 | tf_op jit(solution)/shard_map/all_grads/ppermute | solution.py:181
  79.4 6.1 %collective-permute-done.6 = bf16[2,144,256]{2,1,0:T(8,128)(2,1)S(1)} collective-permute-done((bf16[2,144,256]{2,1,0:T(8,128)(2,1)S(1)}, bf16[2,144,256]{2,1,0:T(8,128)(2,1)S(1)}, u32[]{:S(2)}, u32[]{:S(2)}) %collective-permute-start.6) | collective-permute-done | bytes 147488 | tf_op jit(solution)/shard_map/all_grads/ppermute | solution.py:181
  85.6 5.5 %collective-permute-done.9 = bf16[2,144,256]{2,1,0:T(8,128)(2,1)S(1)} collective-permute-done((bf16[2,144,256]{2,1,0:T(8,128)(2,1)S(1)}, bf16[2,144,256]{2,1,0:T(8,128)(2,1)S(1)}, u32[]{:S(2)}, u32[]{:S(2)}) %collective-permute-start.9) | collective-permute-done | bytes 147488 | tf_op jit(solution)/shard_map/all_grads/ppermute | solution.py:181
  91.0 2.2 collective-permute-done.10
  94.5 11.1 %all-to-all-done.1 = bf16[8,2,64,1536]{3,2,1,0:T(8,128)(2,1)} async-done(((bf16[8,2,64,1536]{3,2,1,0:T(8,128)(2,1)}), bf16[8,2,64,1536]{3,2,1,0:T(8,128)(2,1)}, u32[]{:S(2)}, u32[]{:S(2)}) %all-to-all-start.1) | async-done | bytes 3145760 | tf_op jit(solution)/shard_map/gate_up/all_to_all | solution.py:247
  105.6 2.4 convert_reduce_fusion
  109.0 1.3 broadcast_in_dim.89
  110.3 4.6 %all-to-all-start.2 = ((bf16[8,2,64,768]{3,2,1,0:T(8,128)(2,1)}), bf16[8,2,64,768]{3,2,1,0:T(8,128)(2,1)S(1)}, u32[]{:S(2)}, u32[]{:S(2)}) async-start(bf16[8,2,64,768]{3,2,1,0:T(8,128)(2,1)} %broadcast_in_dim.89), calls=%async_computation.2 | async-start | bytes 3145728 | tf_op jit(solution)/shard_map/gate_up/all_to_all | solution.py:156
  115.3 1.7 fusion.2
  119.2 1.4 reshape.136.gate_ref
  120.5 5.5 %partials.3 = bf16[8,2,64,768]{3,2,1,0:T(8,128)(2,1)} custom-call(bf16[16,2,32,256]{3,2,1,0:T(8,128)(2,1)S(1)} %get-tuple-element.65.g_own_ref.own_ref, bf16[16,2,32,256]{3,2,1,0:T(8,128)(2,1)S(1)} %collective-permute-done.11.g_other_ref.other_ref, bf16[2,768,256]{2,1,0:T(8,128)(2,1)S(1)} %get-tuple-element.50.w_own_ref, ...), custom_call_target="tpu_custom_call" | custom-call | flops 805306368 | bytes 4194304 | tf_op jit(solution)/shard_map/hidden_grad/partials/pallas_call | solution.py:35
  126.0 11.0 %all-to-all-done.2.got_ref = bf16[8,2,64,768]{3,2,1,0:T(8,128)(2,1)S(1)} async-done(((bf16[8,2,64,768]{3,2,1,0:T(8,128)(2,1)}), bf16[8,2,64,768]{3,2,1,0:T(8,128)(2,1)S(1)}, u32[]{:S(2)}, u32[]{:S(2)}) %all-to-all-start.2) | async-done | bytes 1572896 | tf_op jit(solution)/shard_map/gate_up/all_to_all | solution.py:156
  137.0 4.3 %all-to-all-start.3 = ((bf16[8,2,64,768]{3,2,1,0:T(8,128)(2,1)}), bf16[8,2,64,768]{3,2,1,0:T(8,128)(2,1)}, u32[]{:S(2)}, u32[]{:S(2)}) async-start(bf16[8,2,64,768]{3,2,1,0:T(8,128)(2,1)} %partials.3), calls=%async_computation.3 | async-start | bytes 3145728 | tf_op jit(solution)/shard_map/hidden_grad/all_to_all | solution.py:247
  142.4 3.6 %expert_out_kernel.1 = (bf16[16,2,32,256]{3,2,1,0:T(8,128)(2,1)S(1)}, bf16[16,2,32,256]{3,2,1,0:T(8,128)(2,1)S(1)}, f32[2,512,1]{2,1,0:T(8,128)S(1)}) custom-call(bf16[8,2,64,768]{3,2,1,0:T(8,128)(2,1)S(1)} %all-to-all-done.2.got_ref, f32[2,512,1]{2,1,0:T(8,128)S(1)} %copy-done.10, bf16[16,2,32,256]{3,2,1,0:T(8,128)(2,1)S(1)} %get-tuple-element.65.g_own_ref.own_ref, ...), custom_call_target="tpu_custom_call" | custom-call | flops 805306368 | bytes 4194304 | tf_op jit(solution)/shard_map/mixed/expert_out_kernel/pallas_call | solution.py:94
  148.4 1.2 reduce.1
  149.9 1.2 select_reduce_fusion.1
  154.1 8.9 %all-to-all-done.3 = bf16[8,2,64,768]{3,2,1,0:T(8,128)(2,1)} async-done(((bf16[8,2,64,768]{3,2,1,0:T(8,128)(2,1)}), bf16[8,2,64,768]{3,2,1,0:T(8,128)(2,1)}, u32[]{:S(2)}, u32[]{:S(2)}) %all-to-all-start.3) | async-done | bytes 1572896 | tf_op jit(solution)/shard_map/hidden_grad/all_to_all | solution.py:247
  163.0 1.7 convert_reduce_fusion.1
  165.0 1.9 broadcast_in_dim.97
  166.9 3.6 %all-to-all-start.4 = ((bf16[8,2,64,1536]{3,2,1,0:T(8,128)(2,1)}), bf16[8,2,64,1536]{3,2,1,0:T(8,128)(2,1)S(1)}, u32[]{:S(2)}, u32[]{:S(2)}) async-start(bf16[8,2,64,1536]{3,2,1,0:T(8,128)(2,1)} %broadcast_in_dim.97), calls=%async_computation.4 | async-start | bytes 6291456 | tf_op jit(solution)/shard_map/local_grads/all_to_all | solution.py:156
  170.6 2.1 dynamic-slice_bitcast_fusion
  172.8 2.0 collective-permute-start.14
  174.8 2.1 collective-permute-start.15
  176.9 3.0 %collective-permute-start.16 = (bf16[2,136,256]{2,1,0:T(8,128)(2,1)S(1)}, bf16[2,136,256]{2,1,0:T(8,128)(2,1)S(1)}, u32[]{:S(2)}, u32[]{:S(2)}) collective-permute-start(bf16[2,136,256]{2,1,0:T(8,128)(2,1)S(1)} %get-tuple-element.59), channel_id=1, source_target_pairs={{0,8},{1,9},{2,10},{3,11},{4,12},{5,13},{6,14},{7,15},{8,0},{9,1},... | collective-permute-start | bytes 417800 | tf_op jit(solution)/shard_map/mixed/ppermute | solution.py:181
  179.9 1.5 collective-permute-start.17
  181.4 1.4 collective-permute-done.13.refs_1_
  182.8 2.1 collective-permute-start.18
  185.4 8.0 %collective-permute-start.19 = (bf16[2,136,256]{2,1,0:T(8,128)(2,1)S(1)}, bf16[2,136,256]{2,1,0:T(8,128)(2,1)S(1)}, u32[]{:S(2)}, u32[]{:S(2)}) collective-permute-start(bf16[2,136,256]{2,1,0:T(8,128)(2,1)S(1)} %get-tuple-element.56), channel_id=1, source_target_pairs={{0,14},{1,15},{2,0},{3,1},{4,2},{5,3},{6,4},{7,5},{8,6},{9,7},{10,... | collective-permute-start | bytes 417800 | tf_op jit(solution)/shard_map/mixed/ppermute | solution.py:181
  195.4 1.3 copy.70
  196.8 4.4 %collective-permute-done.18.refs_6_ = bf16[2,136,256]{2,1,0:T(8,128)(2,1)S(1)} collective-permute-done((bf16[2,136,256]{2,1,0:T(8,128)(2,1)S(1)}, bf16[2,136,256]{2,1,0:T(8,128)(2,1)S(1)}, u32[]{:S(2)}, u32[]{:S(2)}) %collective-permute-start.18) | collective-permute-done | bytes 139296 | tf_op jit(solution)/shard_map/mixed/ppermute | solution.py:181
  201.2 3.0 %collective-permute-done.19.refs_7_ = bf16[2,136,256]{2,1,0:T(8,128)(2,1)S(1)} collective-permute-done((bf16[2,136,256]{2,1,0:T(8,128)(2,1)S(1)}, bf16[2,136,256]{2,1,0:T(8,128)(2,1)S(1)}, u32[]{:S(2)}, u32[]{:S(2)}) %collective-permute-start.19) | collective-permute-done | bytes 139296 | tf_op jit(solution)/shard_map/mixed/ppermute | solution.py:181
  204.9 2.1 merge.1
  207.0 1.3 collective-permute-start.20
  208.3 3.9 %convolution_convert_fusion.1 = bf16[2,768,512]{2,1,0:T(8,128)(2,1)} fusion(bf16[2,512,768]{2,1,0:T(8,128)(2,1)} %bitcast.88, bf16[2,512,512]{2,1,0:T(8,128)(2,1)} %bitcast.93), kind=kOutput, calls=%fused_computation.8 | convolution fusion | flops 806092800 | bytes 4194304 | tf_op jit(solution)/shard_map/grad_tokens/erf,erd->efd/dot_general | solution.py:326
  212.2 2.3 all-to-all-done.4.got_ref
  214.5 1.4 copy-done.3
  215.9 4.9 %slot_grad_kernel.1 = (bf16[16,2,32,256]{3,2,1,0:T(8,128)(2,1)S(1)}, bf16[16,2,32,256]{3,2,1,0:T(8,128)(2,1)}) custom-call(bf16[8,2,64,1536]{3,2,1,0:T(8,128)(2,1)S(1)} %all-to-all-done.4.got_ref, bf16[2,256,1536]{2,1,0:T(8,128)(2,1)S(1)} %copy-done.3, bf16[2,256,1536]{2,1,0:T(8,128)(2,1)} %collective-permute-done.3.w_other_ref), custom_call_target="tpu_custom_call" | custom-call | flops 1610612736 | bytes 7340032 | tf_op jit(solution)/shard_map/grad_tokens/slot_grad_kernel/pallas_call | solution.py:94
  223.4 1.5 add_convert_fusion.2
  224.9 1.5 fusion.34
  226.5 1.5 add_convert_fusion
  228.0 6.1 %all-to-all-start.5 = ((bf16[16,128,256]{2,1,0:T(8,128)(2,1)}), bf16[16,128,256]{2,1,0:T(8,128)(2,1)}, u32[]{:S(2)}, u32[]{:S(2)}) async-start(bf16[16,128,256]{2,1,0:T(8,128)(2,1)} %add_convert_fusion), calls=%async_computation.5 | async-start | bytes 2097152 | tf_op jit(solution)/shard_map/grad_tokens/all_to_all | solution.py:332
  234.1 1.3 maximum_bitcast_fusion.1
  235.8 1.8 convolution_convert_fusion
  240.2 2.1 collective-permute-done.22
  242.4 5.1 %collective-permute-done.23 = f32[8,128]{1,0:T(8,128)S(1)} collective-permute-done((f32[8,128]{1,0:T(8,128)S(1)}, f32[8,128]{1,0:T(8,128)S(1)}, u32[]{:S(2)}, u32[]{:S(2)}) %collective-permute-start.23) | collective-permute-done | bytes 4128 | tf_op jit(solution)/shard_map/grad_gate/ppermute | solution.py:347
  247.5 1.2 broadcast.126.clone
  249.6 1.4 collective-permute-done.24
  251.9 4.3 %collective-permute-done.25 = f32[8,128]{1,0:T(8,128)S(1)} collective-permute-done((f32[8,128]{1,0:T(8,128)S(1)}, f32[8,128]{1,0:T(8,128)S(1)}, u32[]{:S(2)}, u32[]{:S(2)}) %collective-permute-start.25) | collective-permute-done | bytes 4128 | tf_op jit(solution)/shard_map/grad_gate/ppermute | solution.py:347
  256.9 1.1 slice_dynamic-update-slice_fusion
  258.3 4.1 %all-to-all-done.5 = bf16[16,128,256]{2,1,0:T(8,128)(2,1)} async-done(((bf16[16,128,256]{2,1,0:T(8,128)(2,1)}), bf16[16,128,256]{2,1,0:T(8,128)(2,1)}, u32[]{:S(2)}, u32[]{:S(2)}) %all-to-all-start.5) | async-done | bytes 1048608 | tf_op jit(solution)/shard_map/grad_tokens/all_to_all | solution.py:332
  262.3 2.0 reduce_sum.81
  (188 shorter events, 31.7 us)
Async XLA Ops:
  2.2 11.0 %copy-start.20 = (bf16[4,768,256]{2,1,0:T(8,128)(2,1)S(1)}, bf16[4,768,256]{2,1,0:T(8,128)(2,1)}, u32[]{:S(2)}) copy-start(bf16[4,768,256]{2,1,0:T(8,128)(2,1)} %param.12) | copy-start | bytes 4718596
  3.2 38.8 %all-to-all-start = ((bf16[16,136,256]{2,1,0:T(8,128)(2,1)}), bf16[16,136,256]{2,1,0:T(8,128)(2,1)}, u32[]{:S(2)}, u32[]{:S(2)}) async-start(bf16[16,136,256]{2,1,0:T(8,128)(2,1)} %broadcast_in_dim.88), calls=%async_computation | async-start | bytes 2228224 | tf_op jit(solution)/shard_map/send_tokens/all_to_all | solution.py:156
  13.2 1.0 copy-start.27
  13.2 1.7 copy-start.21
  14.2 4.8 %collective-permute-start.1 = (bf16[2,768,256]{2,1,0:T(8,128)(2,1)}, bf16[2,768,256]{2,1,0:T(8,128)(2,1)}, u32[]{:S(2)}, u32[]{:S(2)}) collective-permute-start(bf16[2,768,256]{2,1,0:T(8,128)(2,1)} %get-tuple-element.51), channel_id=1, source_target_pairs={{0,16},{16,0},{32,48},{48,32},{64,80},{80,64},{96,112},{112,96},{1... | collective-permute-start | bytes 2359304 | tf_op jit(solution)/shard_map/swap_weights/ppermute | solution.py:184
  14.3 1.5 copy-start.22
  14.3 4.8 %collective-permute-start = (bf16[144,256]{1,0:T(8,128)(2,1)S(1)}, bf16[144,256]{1,0:T(8,128)(2,1)S(1)}, u32[]{:S(2)}, u32[]{:S(2)}) collective-permute-start(bf16[144,256]{1,0:T(8,128)(2,1)S(1)} %maximum_maximum_fusion), channel_id=1, source_target_pairs={{0,1},{1,0},{2,3},{3,2},{4,5},{5,4},{6,7},{7,6},{8,9},{9,8},{10,11... | collective-permute-start | bytes 221192 | tf_op jit(solution)/shard_map/send_grads/ppermute | solution.py:207
  17.3 29.9 %copy-start.2 = (bf16[2,256,1536]{2,1,0:T(8,128)(2,1)}, bf16[2,256,1536]{2,1,0:T(8,128)(2,1)S(1)}, u32[]{:S(2)}) copy-start(bf16[2,256,1536]{2,1,0:T(8,128)(2,1)S(1)} %get-tuple-element.45.w_own_ref) | copy-start | bytes 4718596
  17.3 28.0 %collective-permute-start.3 = (bf16[2,256,1536]{2,1,0:T(8,128)(2,1)}, bf16[2,256,1536]{2,1,0:T(8,128)(2,1)}, u32[]{:S(2)}, u32[]{:S(2)}) collective-permute-start(bf16[2,256,1536]{2,1,0:T(8,128)(2,1)} %get-tuple-element.44), channel_id=1, source_target_pairs={{0,16},{16,0},{32,48},{48,32},{64,80},{80,64},{96,112},{112,96},{1... | collective-permute-start | bytes 4718600 | tf_op jit(solution)/shard_map/swap_weights/ppermute | solution.py:184
  19.0 26.1 %copy-start.36 = (bf16[144,256]{1,0:T(8,128)(2,1)}, bf16[144,256]{1,0:T(8,128)(2,1)S(1)}, u32[]{:S(2)}) copy-start(bf16[144,256]{1,0:T(8,128)(2,1)S(1)} %collective-permute-done) | copy-start | bytes 221188
  45.2 2.0 copy-start.6
  45.2 2.0 collective-permute-start.2
  47.2 6.4 %copy-start.9 = (bf16[16,2,32,256]{3,2,1,0:T(8,128)(2,1)}, bf16[16,2,32,256]{3,2,1,0:T(8,128)(2,1)S(1)}, u32[]{:S(2)}) copy-start(bf16[16,2,32,256]{3,2,1,0:T(8,128)(2,1)S(1)} %collective-permute-done.2.other_ref) | copy-start | bytes 1572868
  53.6 6.2 %copy-start.37 = (bf16[144,256]{1,0:T(8,128)(2,1)S(1)}, bf16[144,256]{1,0:T(8,128)(2,1)}, u32[]{:S(2)}) copy-start(bf16[144,256]{1,0:T(8,128)(2,1)} %copy-done.36) | copy-start | bytes 221188
  53.6 52.0 %all-to-all-start.1 = ((bf16[8,2,64,1536]{3,2,1,0:T(8,128)(2,1)}), bf16[8,2,64,1536]{3,2,1,0:T(8,128)(2,1)}, u32[]{:S(2)}, u32[]{:S(2)}) async-start(bf16[8,2,64,1536]{3,2,1,0:T(8,128)(2,1)} %partials.2), calls=%async_computation.1 | async-start | bytes 6291456 | tf_op jit(solution)/shard_map/gate_up/all_to_all | solution.py:247
  59.8 11.9 %collective-permute-start.4 = (bf16[2,144,256]{2,1,0:T(8,128)(2,1)S(1)}, bf16[2,144,256]{2,1,0:T(8,128)(2,1)S(1)}, u32[]{:S(2)}, u32[]{:S(2)}) collective-permute-start(bf16[2,144,256]{2,1,0:T(8,128)(2,1)S(1)} %pad_maximum_fusion.1), channel_id=1, source_target_pairs={{0,2},{1,3},{2,4},{3,5},{4,6},{5,7},{6,8},{7,9},{8,10},{9,11},{10,... | collective-permute-start | bytes 442376 | tf_op jit(solution)/shard_map/all_grads/ppermute | solution.py:181
  60.1 12.5 %collective-permute-start.5 = (bf16[2,144,256]{2,1,0:T(8,128)(2,1)S(1)}, bf16[2,144,256]{2,1,0:T(8,128)(2,1)S(1)}, u32[]{:S(2)}, u32[]{:S(2)}) collective-permute-start(bf16[2,144,256]{2,1,0:T(8,128)(2,1)S(1)} %pad_maximum_fusion.1), channel_id=1, source_target_pairs={{0,4},{1,5},{2,6},{3,7},{4,8},{5,9},{6,10},{7,11},{8,12},{9,13},{1... | collective-permute-start | bytes 442376 | tf_op jit(solution)/shard_map/all_grads/ppermute | solution.py:181
  61.8 23.6 %collective-permute-start.6 = (bf16[2,144,256]{2,1,0:T(8,128)(2,1)S(1)}, bf16[2,144,256]{2,1,0:T(8,128)(2,1)S(1)}, u32[]{:S(2)}, u32[]{:S(2)}) collective-permute-start(bf16[2,144,256]{2,1,0:T(8,128)(2,1)S(1)} %pad_maximum_fusion.1), channel_id=1, source_target_pairs={{0,6},{1,7},{2,8},{3,9},{4,10},{5,11},{6,12},{7,13},{8,14},{9,15},... | collective-permute-start | bytes 442376 | tf_op jit(solution)/shard_map/all_grads/ppermute | solution.py:181
  63.9 21.6 %collective-permute-start.7 = (bf16[2,144,256]{2,1,0:T(8,128)(2,1)S(1)}, bf16[2,144,256]{2,1,0:T(8,128)(2,1)S(1)}, u32[]{:S(2)}, u32[]{:S(2)}) collective-permute-start(bf16[2,144,256]{2,1,0:T(8,128)(2,1)S(1)} %pad_maximum_fusion.1), channel_id=1, source_target_pairs={{0,8},{1,9},{2,10},{3,11},{4,12},{5,13},{6,14},{7,15},{8,0},{9,1},... | collective-permute-start | bytes 442376 | tf_op jit(solution)/shard_map/all_grads/ppermute | solution.py:181
  66.8 18.7 %collective-permute-start.8 = (bf16[2,144,256]{2,1,0:T(8,128)(2,1)S(1)}, bf16[2,144,256]{2,1,0:T(8,128)(2,1)S(1)}, u32[]{:S(2)}, u32[]{:S(2)}) collective-permute-start(bf16[2,144,256]{2,1,0:T(8,128)(2,1)S(1)} %pad_maximum_fusion.1), channel_id=1, source_target_pairs={{0,10},{1,11},{2,12},{3,13},{4,14},{5,15},{6,0},{7,1},{8,2},{9,3},... | collective-permute-start | bytes 442376 | tf_op jit(solution)/shard_map/all_grads/ppermute | solution.py:181
  71.7 19.4 %collective-permute-start.9 = (bf16[2,144,256]{2,1,0:T(8,128)(2,1)S(1)}, bf16[2,144,256]{2,1,0:T(8,128)(2,1)S(1)}, u32[]{:S(2)}, u32[]{:S(2)}) collective-permute-start(bf16[2,144,256]{2,1,0:T(8,128)(2,1)S(1)} %pad_maximum_fusion.1), channel_id=1, source_target_pairs={{0,12},{1,13},{2,14},{3,15},{4,0},{5,1},{6,2},{7,3},{8,4},{9,5},{1... | collective-permute-start | bytes 442376 | tf_op jit(solution)/shard_map/all_grads/ppermute | solution.py:181
  72.6 20.6 %collective-permute-start.10 = (bf16[2,144,256]{2,1,0:T(8,128)(2,1)S(1)}, bf16[2,144,256]{2,1,0:T(8,128)(2,1)S(1)}, u32[]{:S(2)}, u32[]{:S(2)}) collective-permute-start(bf16[2,144,256]{2,1,0:T(8,128)(2,1)S(1)} %pad_maximum_fusion.1), channel_id=1, source_target_pairs={{0,14},{1,15},{2,0},{3,1},{4,2},{5,3},{6,4},{7,5},{8,6},{9,7},{10,... | collective-permute-start | bytes 442376 | tf_op jit(solution)/shard_map/all_grads/ppermute | solution.py:181
  110.3 26.7 %all-to-all-start.2 = ((bf16[8,2,64,768]{3,2,1,0:T(8,128)(2,1)}), bf16[8,2,64,768]{3,2,1,0:T(8,128)(2,1)S(1)}, u32[]{:S(2)}, u32[]{:S(2)}) async-start(bf16[8,2,64,768]{3,2,1,0:T(8,128)(2,1)} %broadcast_in_dim.89), calls=%async_computation.2 | async-start | bytes 3145728 | tf_op jit(solution)/shard_map/gate_up/all_to_all | solution.py:156
  118.2 23.1 %copy-start.4 = (bf16[16,2,32,256]{3,2,1,0:T(8,128)(2,1)}, bf16[16,2,32,256]{3,2,1,0:T(8,128)(2,1)S(1)}, u32[]{:S(2)}) copy-start(bf16[16,2,32,256]{3,2,1,0:T(8,128)(2,1)S(1)} %get-tuple-element.65.g_own_ref.own_ref) | copy-start | bytes 1572868
  118.2 2.3 collective-permute-start.11
  120.5 20.8 %copy-start.7 = (bf16[16,2,32,256]{3,2,1,0:T(8,128)(2,1)}, bf16[16,2,32,256]{3,2,1,0:T(8,128)(2,1)S(1)}, u32[]{:S(2)}) copy-start(bf16[16,2,32,256]{3,2,1,0:T(8,128)(2,1)S(1)} %collective-permute-done.11.g_other_ref.other_ref) | copy-start | bytes 1572868
  137.0 4.3 %copy-start = (bf16[8,2,64,768]{3,2,1,0:T(8,128)(2,1)}, bf16[8,2,64,768]{3,2,1,0:T(8,128)(2,1)S(1)}, u32[]{:S(2)}) copy-start(bf16[8,2,64,768]{3,2,1,0:T(8,128)(2,1)S(1)} %all-to-all-done.2.got_ref) | copy-start | bytes 4718596
  137.0 26.0 %all-to-all-start.3 = ((bf16[8,2,64,768]{3,2,1,0:T(8,128)(2,1)}), bf16[8,2,64,768]{3,2,1,0:T(8,128)(2,1)}, u32[]{:S(2)}, u32[]{:S(2)}) async-start(bf16[8,2,64,768]{3,2,1,0:T(8,128)(2,1)} %partials.3), calls=%async_computation.3 | async-start | bytes 3145728 | tf_op jit(solution)/shard_map/hidden_grad/all_to_all | solution.py:247
  141.4 1.0 copy-start.10
  149.8 2.7 %copy-start.13 = (bf16[16,2,32,256]{3,2,1,0:T(8,128)(2,1)S(1)}, bf16[16,2,32,256]{3,2,1,0:T(8,128)(2,1)}, u32[]{:S(2)}) copy-start(bf16[16,2,32,256]{3,2,1,0:T(8,128)(2,1)} %copy-done.12) | copy-start | bytes 1572868
  149.8 2.2 collective-permute-start.12
  153.0 11.7 %copy-start.18 = (f32[2,64,1536]{2,1,0:T(8,128)S(1)}, f32[2,64,1536]{2,1,0:T(8,128)}, u32[]{:S(2)}) copy-start(f32[2,64,1536]{2,1,0:T(8,128)} %copy-done.17) | copy-start | bytes 2359300
  166.9 47.6 %all-to-all-start.4 = ((bf16[8,2,64,1536]{3,2,1,0:T(8,128)(2,1)}), bf16[8,2,64,1536]{3,2,1,0:T(8,128)(2,1)S(1)}, u32[]{:S(2)}, u32[]{:S(2)}) async-start(bf16[8,2,64,1536]{3,2,1,0:T(8,128)(2,1)} %broadcast_in_dim.97), calls=%async_computation.4 | async-start | bytes 6291456 | tf_op jit(solution)/shard_map/local_grads/all_to_all | solution.py:156
  170.6 22.9 %copy-start.5 = (bf16[16,2,32,256]{3,2,1,0:T(8,128)(2,1)S(1)}, bf16[16,2,32,256]{3,2,1,0:T(8,128)(2,1)}, u32[]{:S(2)}) copy-start(bf16[16,2,32,256]{3,2,1,0:T(8,128)(2,1)} %copy-done.4) | copy-start | bytes 1572868
  170.6 22.9 %copy-start.8 = (bf16[16,2,32,256]{3,2,1,0:T(8,128)(2,1)S(1)}, bf16[16,2,32,256]{3,2,1,0:T(8,128)(2,1)}, u32[]{:S(2)}) copy-start(bf16[16,2,32,256]{3,2,1,0:T(8,128)(2,1)} %copy-done.7) | copy-start | bytes 1572868
  172.8 10.0 %collective-permute-start.13 = (bf16[2,136,256]{2,1,0:T(8,128)(2,1)S(1)}, bf16[2,136,256]{2,1,0:T(8,128)(2,1)S(1)}, u32[]{:S(2)}, u32[]{:S(2)}) collective-permute-start(bf16[2,136,256]{2,1,0:T(8,128)(2,1)S(1)} %get-tuple-element.62), channel_id=1, source_target_pairs={{0,2},{1,3},{2,4},{3,5},{4,6},{5,7},{6,8},{7,9},{8,10},{9,11},{10,... | collective-permute-start | bytes 417800 | tf_op jit(solution)/shard_map/mixed/ppermute | solution.py:181
  172.8 12.6 %collective-permute-start.14 = (bf16[2,136,256]{2,1,0:T(8,128)(2,1)S(1)}, bf16[2,136,256]{2,1,0:T(8,128)(2,1)S(1)}, u32[]{:S(2)}, u32[]{:S(2)}) collective-permute-start(bf16[2,136,256]{2,1,0:T(8,128)(2,1)S(1)} %get-tuple-element.61), channel_id=1, source_target_pairs={{0,4},{1,5},{2,6},{3,7},{4,8},{5,9},{6,10},{7,11},{8,12},{9,13},{1... | collective-permute-start | bytes 417800 | tf_op jit(solution)/shard_map/mixed/ppermute | solution.py:181
  174.8 21.9 %collective-permute-start.15 = (bf16[2,136,256]{2,1,0:T(8,128)(2,1)S(1)}, bf16[2,136,256]{2,1,0:T(8,128)(2,1)S(1)}, u32[]{:S(2)}, u32[]{:S(2)}) collective-permute-start(bf16[2,136,256]{2,1,0:T(8,128)(2,1)S(1)} %get-tuple-element.60), channel_id=1, source_target_pairs={{0,6},{1,7},{2,8},{3,9},{4,10},{5,11},{6,12},{7,13},{8,14},{9,15},... | collective-permute-start | bytes 417800 | tf_op jit(solution)/shard_map/mixed/ppermute | solution.py:181
  176.9 19.8 %collective-permute-start.16 = (bf16[2,136,256]{2,1,0:T(8,128)(2,1)S(1)}, bf16[2,136,256]{2,1,0:T(8,128)(2,1)S(1)}, u32[]{:S(2)}, u32[]{:S(2)}) collective-permute-start(bf16[2,136,256]{2,1,0:T(8,128)(2,1)S(1)} %get-tuple-element.59), channel_id=1, source_target_pairs={{0,8},{1,9},{2,10},{3,11},{4,12},{5,13},{6,14},{7,15},{8,0},{9,1},... | collective-permute-start | bytes 417800 | tf_op jit(solution)/shard_map/mixed/ppermute | solution.py:181
  179.9 16.9 %collective-permute-start.17 = (bf16[2,136,256]{2,1,0:T(8,128)(2,1)S(1)}, bf16[2,136,256]{2,1,0:T(8,128)(2,1)S(1)}, u32[]{:S(2)}, u32[]{:S(2)}) collective-permute-start(bf16[2,136,256]{2,1,0:T(8,128)(2,1)S(1)} %get-tuple-element.58), channel_id=1, source_target_pairs={{0,10},{1,11},{2,12},{3,13},{4,14},{5,15},{6,0},{7,1},{8,2},{9,3},... | collective-permute-start | bytes 417800 | tf_op jit(solution)/shard_map/mixed/ppermute | solution.py:181
  182.8 11.9 %copy-start.28 = (bf16[2,136,256]{2,1,0:T(8,128)(2,1)}, bf16[2,136,256]{2,1,0:T(8,128)(2,1)S(1)}, u32[]{:S(2)}) copy-start(bf16[2,136,256]{2,1,0:T(8,128)(2,1)S(1)} %collective-permute-done.13.refs_1_) | copy-start | bytes 417796
  182.8 18.4 %collective-permute-start.18 = (bf16[2,136,256]{2,1,0:T(8,128)(2,1)S(1)}, bf16[2,136,256]{2,1,0:T(8,128)(2,1)S(1)}, u32[]{:S(2)}, u32[]{:S(2)}) collective-permute-start(bf16[2,136,256]{2,1,0:T(8,128)(2,1)S(1)} %get-tuple-element.57), channel_id=1, source_target_pairs={{0,12},{1,13},{2,14},{3,15},{4,0},{5,1},{6,2},{7,3},{8,4},{9,5},{1... | collective-permute-start | bytes 417800 | tf_op jit(solution)/shard_map/mixed/ppermute | solution.py:181
  185.4 8.1 %copy-start.29 = (bf16[2,136,256]{2,1,0:T(8,128)(2,1)}, bf16[2,136,256]{2,1,0:T(8,128)(2,1)S(1)}, u32[]{:S(2)}) copy-start(bf16[2,136,256]{2,1,0:T(8,128)(2,1)S(1)} %collective-permute-done.14.refs_2_) | copy-start | bytes 417796
  185.4 18.8 %collective-permute-start.19 = (bf16[2,136,256]{2,1,0:T(8,128)(2,1)S(1)}, bf16[2,136,256]{2,1,0:T(8,128)(2,1)S(1)}, u32[]{:S(2)}, u32[]{:S(2)}) collective-permute-start(bf16[2,136,256]{2,1,0:T(8,128)(2,1)S(1)} %get-tuple-element.56), channel_id=1, source_target_pairs={{0,14},{1,15},{2,0},{3,1},{4,2},{5,3},{6,4},{7,5},{8,6},{9,7},{10,... | collective-permute-start | bytes 417800 | tf_op jit(solution)/shard_map/mixed/ppermute | solution.py:181
  193.6 1.8 copy-start.1
  196.7 7.5 %copy-start.30 = (bf16[2,136,256]{2,1,0:T(8,128)(2,1)}, bf16[2,136,256]{2,1,0:T(8,128)(2,1)S(1)}, u32[]{:S(2)}) copy-start(bf16[2,136,256]{2,1,0:T(8,128)(2,1)S(1)} %collective-permute-done.15.refs_3_) | copy-start | bytes 417796
  196.7 7.5 %copy-start.31 = (bf16[2,136,256]{2,1,0:T(8,128)(2,1)}, bf16[2,136,256]{2,1,0:T(8,128)(2,1)S(1)}, u32[]{:S(2)}) copy-start(bf16[2,136,256]{2,1,0:T(8,128)(2,1)S(1)} %collective-permute-done.16.refs_4_) | copy-start | bytes 417796
  196.8 7.4 %copy-start.32 = (bf16[2,136,256]{2,1,0:T(8,128)(2,1)}, bf16[2,136,256]{2,1,0:T(8,128)(2,1)S(1)}, u32[]{:S(2)}) copy-start(bf16[2,136,256]{2,1,0:T(8,128)(2,1)S(1)} %collective-permute-done.17.refs_5_) | copy-start | bytes 417796
  201.2 3.0 %copy-start.33 = (bf16[2,136,256]{2,1,0:T(8,128)(2,1)}, bf16[2,136,256]{2,1,0:T(8,128)(2,1)S(1)}, u32[]{:S(2)}) copy-start(bf16[2,136,256]{2,1,0:T(8,128)(2,1)S(1)} %collective-permute-done.18.refs_6_) | copy-start | bytes 417796
  207.0 5.2 %collective-permute-start.20 = (bf16[192,256]{1,0:T(8,128)(2,1)}, bf16[192,256]{1,0:T(8,128)(2,1)S(1)}, u32[]{:S(2)}, u32[]{:S(2)}) collective-permute-start(bf16[192,256]{1,0:T(8,128)(2,1)} %get-tuple-element.30), channel_id=1, source_target_pairs={{0,1},{1,0},{2,3},{3,2},{4,5},{5,4},{6,7},{7,6},{8,9},{9,8},{10,11... | collective-permute-start | bytes 294920 | tf_op jit(solution)/shard_map/mixed/ppermute | solution.py:314
  212.2 8.7 %copy-start.35 = (bf16[192,256]{1,0:T(8,128)(2,1)}, bf16[192,256]{1,0:T(8,128)(2,1)S(1)}, u32[]{:S(2)}) copy-start(bf16[192,256]{1,0:T(8,128)(2,1)S(1)} %collective-permute-done.20) | copy-start | bytes 294916
  214.5 1.4 copy-start.3
  221.7 3.3 %collective-permute-start.21 = (bf16[16,2,32,256]{3,2,1,0:T(8,128)(2,1)}, bf16[16,2,32,256]{3,2,1,0:T(8,128)(2,1)}, u32[]{:S(2)}, u32[]{:S(2)}) collective-permute-start(bf16[16,2,32,256]{3,2,1,0:T(8,128)(2,1)} %get-tuple-element.36), channel_id=1, source_target_pairs={{0,16},{16,0},{32,48},{48,32},{64,80},{80,64},{96,112},{112,96},{1... | collective-permute-start | bytes 1572872 | tf_op jit(solution)/shard_map/grad_tokens/ppermute | solution.py:184
  222.6 3.9 %copy-start.15 = (bf16[16,2,32,256]{3,2,1,0:T(8,128)(2,1)S(1)}, bf16[16,2,32,256]{3,2,1,0:T(8,128)(2,1)}, u32[]{:S(2)}) copy-start(bf16[16,2,32,256]{3,2,1,0:T(8,128)(2,1)} %copy-done.14) | copy-start | bytes 1572868
  228.0 34.3 %all-to-all-start.5 = ((bf16[16,128,256]{2,1,0:T(8,128)(2,1)}), bf16[16,128,256]{2,1,0:T(8,128)(2,1)}, u32[]{:S(2)}, u32[]{:S(2)}) async-start(bf16[16,128,256]{2,1,0:T(8,128)(2,1)} %add_convert_fusion), calls=%async_computation.5 | async-start | bytes 2097152 | tf_op jit(solution)/shard_map/grad_tokens/all_to_all | solution.py:332
  237.7 1.4 copy-start.25
  237.7 19.1 %collective-permute-start.26 = (bf16[2,256,1536]{2,1,0:T(8,128)(2,1)S(1)}, bf16[2,256,1536]{2,1,0:T(8,128)(2,1)S(1)}, u32[]{:S(2)}, u32[]{:S(2)}) collective-permute-start(bf16[2,256,1536]{2,1,0:T(8,128)(2,1)S(1)} %slice.140), channel_id=1, source_target_pairs={{0,16},{16,0},{32,48},{48,32},{64,80},{80,64},{96,112},{112,96},{1... | collective-permute-start | bytes 4718600 | tf_op jit(solution)/shard_map/weight_grads/ppermute | solution.py:184
  239.2 17.6 %collective-permute-start.27 = (bf16[2,768,256]{2,1,0:T(8,128)(2,1)S(1)}, bf16[2,768,256]{2,1,0:T(8,128)(2,1)S(1)}, u32[]{:S(2)}, u32[]{:S(2)}) collective-permute-start(bf16[2,768,256]{2,1,0:T(8,128)(2,1)S(1)} %get-tuple-element.46), channel_id=1, source_target_pairs={{0,16},{16,0},{32,48},{48,32},{64,80},{80,64},{96,112},{112,96},{1... | collective-permute-start | bytes 2359304 | tf_op jit(solution)/shard_map/weight_grads/ppermute | solution.py:184
  239.9 2.4 collective-permute-start.22
  242.4 5.1 %collective-permute-start.23 = (f32[8,128]{1,0:T(8,128)S(1)}, f32[8,128]{1,0:T(8,128)S(1)}, u32[]{:S(2)}, u32[]{:S(2)}) collective-permute-start(f32[8,128]{1,0:T(8,128)S(1)} %add.317), channel_id=1, source_target_pairs={{0,32},{16,48},{32,0},{48,16},{64,96},{80,112},{96,64},{112,80},{1... | collective-permute-start | bytes 12296 | tf_op jit(solution)/shard_map/grad_gate/ppermute | solution.py:347
  247.5 3.6 %collective-permute-start.24 = (f32[8,128]{1,0:T(8,128)S(1)}, f32[8,128]{1,0:T(8,128)S(1)}, u32[]{:S(2)}, u32[]{:S(2)}) collective-permute-start(f32[8,128]{1,0:T(8,128)S(1)} %add.318), channel_id=1, source_target_pairs={{0,64},{16,80},{32,96},{48,112},{64,0},{80,16},{96,32},{112,48},{1... | collective-permute-start | bytes 12296 | tf_op jit(solution)/shard_map/grad_gate/ppermute | solution.py:347
  251.1 5.1 %collective-permute-start.25 = (f32[8,128]{1,0:T(8,128)S(1)}, f32[8,128]{1,0:T(8,128)S(1)}, u32[]{:S(2)}, u32[]{:S(2)}) collective-permute-start(f32[8,128]{1,0:T(8,128)S(1)} %add.319), channel_id=1, source_target_pairs={{0,128},{16,144},{32,160},{48,176},{64,192},{80,208},{96,224},{112... | collective-permute-start | bytes 12296 | tf_op jit(solution)/shard_map/grad_gate/ppermute | solution.py:347
  256.8 1.4 copy-start.23
  258.3 6.1 %copy-start.24 = (bf16[4,256,768]{2,1,0:T(8,128)(2,1)}, bf16[4,256,768]{2,1,0:T(8,128)(2,1)S(1)}, u32[]{:S(2)}) copy-start(bf16[4,256,768]{2,1,0:T(8,128)(2,1)S(1)} %get-tuple-element.49) | copy-start | bytes 4718596
  (10 other events, 8.3 us)

commit v3 on v2

--- a/solution.py
+++ b/solution.py
@@ -25,7 +25,7 @@
 def partials(own, other, w_own, w_other, chips, width_last):
     blocks, half, cap, width = own.shape
     wide = w_own.shape[1] if width_last else w_own.shape[2]
-    tile = wide // 3 if wide % 384 == 0 else wide
+    tile = wide // 2 if wide % 256 == 0 else wide
     rows = blocks * cap
     row_spec = pl.BlockSpec((blocks, 1, cap, width), lambda e, f: (0, e, 0, 0))
     if width_last:
@@ -76,15 +76,16 @@
 
 
 def per_expert(kernel, got, w_own, w_other, cap, width_last, gates=None, grads=()):
+    split = 1 if gates is None else 2
     chips, half, share, wide = got.shape
     width = w_own.shape[1] if width_last else w_own.shape[2]
     rows = chips * share
     w_spec = pl.BlockSpec((1,) + w_own.shape[1:], lambda e, p: (e, 0, 0))
-    row_spec = pl.BlockSpec((rows // cap // 2, 1, cap, width), lambda e, p: (p, e, 0, 0))
-    column_spec = pl.BlockSpec((1, rows // 2, 1), lambda e, p: (e, p, 0))
+    row_spec = pl.BlockSpec((rows // cap // split, 1, cap, width), lambda e, p: (p, e, 0, 0))
+    column_spec = pl.BlockSpec((1, rows // split, 1), lambda e, p: (e, p, 0))
     outs = [jax.ShapeDtypeStruct((rows // cap, half, cap, width), got.dtype)] * 2
     out_specs = [row_spec, row_spec]
-    in_specs = [pl.BlockSpec((chips // 2, 1, share, wide), lambda e, p: (p, e, 0, 0))]
+    in_specs = [pl.BlockSpec((chips // split, 1, share, wide), lambda e, p: (p, e, 0, 0))]
     args = [got]
     if gates is not None:
         in_specs = in_specs + [column_spec, row_spec, row_spec]
@@ -94,7 +95,7 @@
     return pl.pallas_call(
         kernel,
         out_shape=outs,
-        grid=(half, 2),
+        grid=(half, split),
         in_specs=in_specs + [w_spec, w_spec],
         out_specs=out_specs,
         cost_estimate=pl.CostEstimate(
@@ -310,9 +311,12 @@
             return lax.dynamic_index_in_dim(by_level, (level + step) % levels, 0, keepdims=False)
 
         arrived = [at_level(0)] + [shifted(at_level(step), step) for step in range(1, levels)]
+        g_rows = join_rows(g_mine, g_theirs)
+        all_hidden = in_rows(after(got_hidden, arrived[1]))
+        dd = jnp.einsum("erf,erd->efd", all_hidden, g_rows, preferred_element_type=f32).astype(bf16)
+        arrived[0] = after(arrived[0], dd)
         keep, give = merge((col % 2).astype(jnp.int32), arrived, extra)
         take = lax.ppermute(give, "expert", [(i, i ^ 1) for i in range(cols)])
-        mixed = (keep[:tok].astype(f32) + take[:tok].astype(f32)).astype(bf16)
 
     with jax.named_scope("local_grads"):
         gate_grad = (hidden_grad * up_pre * sigmoid_g * (1.0 + gate_pre * (1.0 - sigmoid_g))).astype(bf16)
@@ -321,14 +325,13 @@
         got_grads = spread(local_grads, "dp", chips, same_core)
 
     with jax.named_scope("grad_tokens"):
-        g_rows = join_rows(g_mine, g_theirs)
-        all_hidden = in_rows(after(got_hidden, mixed_parts))
-        dd = jnp.einsum("erf,erd->efd", all_hidden, g_rows, preferred_element_type=f32).astype(bf16)
-        got_grads = after(got_grads, (take, dd))
+        got_grads = after(got_grads, take)
         slot_own, slot_other = per_expert(
             slot_grad_kernel, got_grads, wgu_mine, wgu_theirs, cap, True
         )
-        grad_parts = after(combine(slot_own, swap(slot_other)), mixed)
+        grad_parts = combine(slot_own, swap(slot_other))
+        keep, take = after((keep, take), grad_parts)
+        mixed = (keep[:tok].astype(f32) + take[:tok].astype(f32)).astype(bf16)
         back = lax.all_to_all(grad_parts, "expert", 0, 0, tiled=True)
         grad_tokens = jnp.sum(back.astype(f32), axis=0).astype(bf16)
         gu_grads = in_rows(after(got_grads, grad_parts))

time: 266 us -> 263 us (0.989)
  waiting for transfers between devices: 104 us -> 112 us
  local copies, waits for them, and re-layouts: 32.4 us -> 28.8 us
    ppermute x1, waiting for transfers between devices: 0.01 us -> 3.56 us  [on_device(): take = lax.ppermute(give, 'expert', [(i, i ^ 1) for i in range(cols)])]
    ppermute x1, waiting for transfers between devices: 1.27 us -> 4.77 us  [on_device(): lax.ppermute(own_grads, 'expert', [(i, i ^ 1) for i in range(cols)])]
    unnamed x82 -> x84, local copies, waits for them, and re-layouts: 12.5 us -> 12.6 us
  transfers between devices with their start and end apart: 34 -> 34, of which waited for: 23 -> 24; matrix products, arithmetic and copies ran while one was open for 13% -> 11% of each run, Pallas kernels for 4% -> 4%
where the time goes in v3:
time: 263 us; the launch traced here: 262 us
  waiting for transfers between devices  112 us (43%)
  starting transfers between devices  72.4 us (28%)
  local copies, waits for them, and re-layouts  28.8 us (11%)
  Pallas kernels  20 us (8%)
  other arithmetic  15.7 us (6%)
  matrix products  11.4 us (4%)
    ppermute x14, starting transfers between devices, shifted(): return lax.ppermute(value, 'expert', steps)  35.3 us
    all_to_all x3, waiting for transfers between devices, spread(): lax.all_to_all(copies, axis_name, 0, 0, tiled=True, axis_index_groups=gro...  34.1 us
    ppermute x14, waiting for transfers between devices, shifted(): return lax.ppermute(value, 'expert', steps)  26.8 us
    all_to_all x2, waiting for transfers between devices, shares(): lax.all_to_all(part, 'dp', 0, 0, tiled=True, axis_index_groups=same_core)  21.2 us
    all_to_all x3, starting transfers between devices, spread(): lax.all_to_all(copies, axis_name, 0, 0, tiled=True, axis_index_groups=gro...  18.1 us
    unnamed x84, local copies, waits for them, and re-layouts  12.6 us
    ppermute x4, waiting for transfers between devices, on_device(): lax.ppermute(gate_sum, 'dp', [(i, i ^ bit) for i in range(parties)])  12.2 us
    all_to_all x2, starting transfers between devices, shares(): lax.all_to_all(part, 'dp', 0, 0, tiled=True, axis_index_groups=same_core)  10.5 us
  transfers between devices with their start and end apart: 34, of which 24 were waited for; matrix products, arithmetic and copies ran while one was open for 11% of the time, Pallas kernels for 4%

profile of v3, /device:TPU:8, one launch (start us, length us, event | category | flops | bytes accessed | tf_op | source)
XLA Modules:
  0.0 262.0 jit_solution(15369521121542714342)
XLA Ops:
  3.2 9.9 %all-to-all-start = ((bf16[16,136,256]{2,1,0:T(8,128)(2,1)}), bf16[16,136,256]{2,1,0:T(8,128)(2,1)}, u32[]{:S(2)}, u32[]{:S(2)}) async-start(bf16[16,136,256]{2,1,0:T(8,128)(2,1)} %broadcast_in_dim.88), calls=%async_computation | async-start | bytes 2228224 | tf_op jit(solution)/shard_map/send_tokens/all_to_all | solution.py:157
  15.9 1.4 constant_dynamic-slice_fusion.4
  17.6 4.8 %collective-permute-done = bf16[144,256]{1,0:T(8,128)(2,1)S(1)} collective-permute-done((bf16[144,256]{1,0:T(8,128)(2,1)S(1)}, bf16[144,256]{1,0:T(8,128)(2,1)S(1)}, u32[]{:S(2)}, u32[]{:S(2)}) %collective-permute-start) | collective-permute-done | bytes 73760 | tf_op jit(solution)/shard_map/send_grads/ppermute | solution.py:208
  22.4 19.6 %all-to-all-done = bf16[16,136,256]{2,1,0:T(8,128)(2,1)} async-done(((bf16[16,136,256]{2,1,0:T(8,128)(2,1)}), bf16[16,136,256]{2,1,0:T(8,128)(2,1)}, u32[]{:S(2)}, u32[]{:S(2)}) %all-to-all-start) | async-done | bytes 1114144 | tf_op jit(solution)/shard_map/send_tokens/all_to_all | solution.py:157
  43.4 1.7 convolution_convert_fusion.2
  45.3 1.9 collective-permute-done.2.other_ref
  47.2 5.2 %partials.2 = bf16[8,2,64,1536]{3,2,1,0:T(8,128)(2,1)} custom-call(bf16[16,2,32,256]{3,2,1,0:T(8,128)(2,1)S(1)} %get-tuple-element.43.own_ref, bf16[16,2,32,256]{3,2,1,0:T(8,128)(2,1)S(1)} %collective-permute-done.2.other_ref, bf16[2,256,1536]{2,1,0:T(8,128)(2,1)S(1)} %get-tuple-element.49.w_own_ref, bf16[2,256,1536]{2,1,0:T(8,128)(2,1)} %collective-permute-done.3.w_other_ref), custom_call_target="tpu_custom_call" | custom-call | flops 1610612736 | bytes 7340032 | tf_op jit(solution)/shard_map/gate_up/partials/pallas_call | solution.py:35
  53.2 6.2 %all-to-all-start.1 = ((bf16[8,2,64,1536]{3,2,1,0:T(8,128)(2,1)}), bf16[8,2,64,1536]{3,2,1,0:T(8,128)(2,1)}, u32[]{:S(2)}, u32[]{:S(2)}) async-start(bf16[8,2,64,1536]{3,2,1,0:T(8,128)(2,1)} %partials.2), calls=%async_computation.1 | async-start | bytes 6291456 | tf_op jit(solution)/shard_map/gate_up/all_to_all | solution.py:248
  59.8 1.8 collective-permute-start.5
  61.5 2.0 collective-permute-start.6
  63.6 3.0 %collective-permute-start.7 = (bf16[2,144,256]{2,1,0:T(8,128)(2,1)S(1)}, bf16[2,144,256]{2,1,0:T(8,128)(2,1)S(1)}, u32[]{:S(2)}, u32[]{:S(2)}) collective-permute-start(bf16[2,144,256]{2,1,0:T(8,128)(2,1)S(1)} %pad_maximum_fusion.1), channel_id=1, source_target_pairs={{0,8},{1,9},{2,10},{3,11},{4,12},{5,13},{6,14},{7,15},{8,0},{9,1},... | collective-permute-start | bytes 442376 | tf_op jit(solution)/shard_map/all_grads/ppermute | solution.py:182
  66.5 1.8 collective-permute-start.8
  68.4 2.9 %collective-permute-done.4 = bf16[2,144,256]{2,1,0:T(8,128)(2,1)S(1)} collective-permute-done((bf16[2,144,256]{2,1,0:T(8,128)(2,1)S(1)}, bf16[2,144,256]{2,1,0:T(8,128)(2,1)S(1)}, u32[]{:S(2)}, u32[]{:S(2)}) %collective-permute-start.4) | collective-permute-done | bytes 147488 | tf_op jit(solution)/shard_map/all_grads/ppermute | solution.py:182
  72.3 6.8 %collective-permute-start.10 = (bf16[2,144,256]{2,1,0:T(8,128)(2,1)S(1)}, bf16[2,144,256]{2,1,0:T(8,128)(2,1)S(1)}, u32[]{:S(2)}, u32[]{:S(2)}) collective-permute-start(bf16[2,144,256]{2,1,0:T(8,128)(2,1)S(1)} %pad_maximum_fusion.1), channel_id=1, source_target_pairs={{0,14},{1,15},{2,0},{3,1},{4,2},{5,3},{6,4},{7,5},{8,6},{9,7},{10,... | collective-permute-start | bytes 442376 | tf_op jit(solution)/shard_map/all_grads/ppermute | solution.py:182
  79.0 6.1 %collective-permute-done.6 = bf16[2,144,256]{2,1,0:T(8,128)(2,1)S(1)} collective-permute-done((bf16[2,144,256]{2,1,0:T(8,128)(2,1)S(1)}, bf16[2,144,256]{2,1,0:T(8,128)(2,1)S(1)}, u32[]{:S(2)}, u32[]{:S(2)}) %collective-permute-start.6) | collective-permute-done | bytes 147488 | tf_op jit(solution)/shard_map/all_grads/ppermute | solution.py:182
  85.2 5.5 %collective-permute-done.9 = bf16[2,144,256]{2,1,0:T(8,128)(2,1)S(1)} collective-permute-done((bf16[2,144,256]{2,1,0:T(8,128)(2,1)S(1)}, bf16[2,144,256]{2,1,0:T(8,128)(2,1)S(1)}, u32[]{:S(2)}, u32[]{:S(2)}) %collective-permute-start.9) | collective-permute-done | bytes 147488 | tf_op jit(solution)/shard_map/all_grads/ppermute | solution.py:182
  90.7 2.2 collective-permute-done.10
  94.2 11.1 %all-to-all-done.1 = bf16[8,2,64,1536]{3,2,1,0:T(8,128)(2,1)} async-done(((bf16[8,2,64,1536]{3,2,1,0:T(8,128)(2,1)}), bf16[8,2,64,1536]{3,2,1,0:T(8,128)(2,1)}, u32[]{:S(2)}, u32[]{:S(2)}) %all-to-all-start.1) | async-done | bytes 3145760 | tf_op jit(solution)/shard_map/gate_up/all_to_all | solution.py:248
  105.3 2.4 convert_reduce_fusion
  108.7 1.3 broadcast_in_dim.89
  110.0 4.6 %all-to-all-start.2 = ((bf16[8,2,64,768]{3,2,1,0:T(8,128)(2,1)}), bf16[8,2,64,768]{3,2,1,0:T(8,128)(2,1)S(1)}, u32[]{:S(2)}, u32[]{:S(2)}) async-start(bf16[8,2,64,768]{3,2,1,0:T(8,128)(2,1)} %broadcast_in_dim.89), calls=%async_computation.2 | async-start | bytes 3145728 | tf_op jit(solution)/shard_map/gate_up/all_to_all | solution.py:157
  115.0 1.7 fusion.2
  118.9 1.4 reshape.136.gate_ref
  120.2 4.5 %partials.3 = bf16[8,2,64,768]{3,2,1,0:T(8,128)(2,1)} custom-call(bf16[16,2,32,256]{3,2,1,0:T(8,128)(2,1)S(1)} %get-tuple-element.69.g_own_ref.own_ref, bf16[16,2,32,256]{3,2,1,0:T(8,128)(2,1)S(1)} %collective-permute-done.11.g_other_ref.other_ref, bf16[2,768,256]{2,1,0:T(8,128)(2,1)S(1)} %get-tuple-element.54.w_own_ref, ...), custom_call_target="tpu_custom_call" | custom-call | flops 805306368 | bytes 4194304 | tf_op jit(solution)/shard_map/hidden_grad/partials/pallas_call | solution.py:35
  124.7 12.0 %all-to-all-done.2.got_ref = bf16[8,2,64,768]{3,2,1,0:T(8,128)(2,1)S(1)} async-done(((bf16[8,2,64,768]{3,2,1,0:T(8,128)(2,1)}), bf16[8,2,64,768]{3,2,1,0:T(8,128)(2,1)S(1)}, u32[]{:S(2)}, u32[]{:S(2)}) %all-to-all-start.2) | async-done | bytes 1572896 | tf_op jit(solution)/shard_map/gate_up/all_to_all | solution.py:157
  136.7 4.3 %all-to-all-start.3 = ((bf16[8,2,64,768]{3,2,1,0:T(8,128)(2,1)}), bf16[8,2,64,768]{3,2,1,0:T(8,128)(2,1)}, u32[]{:S(2)}, u32[]{:S(2)}) async-start(bf16[8,2,64,768]{3,2,1,0:T(8,128)(2,1)} %partials.3), calls=%async_computation.3 | async-start | bytes 3145728 | tf_op jit(solution)/shard_map/hidden_grad/all_to_all | solution.py:248
  142.1 4.2 %expert_out_kernel.1 = (bf16[16,2,32,256]{3,2,1,0:T(8,128)(2,1)S(1)}, bf16[16,2,32,256]{3,2,1,0:T(8,128)(2,1)}, f32[2,512,1]{2,1,0:T(8,128)S(1)}) custom-call(bf16[8,2,64,768]{3,2,1,0:T(8,128)(2,1)S(1)} %all-to-all-done.2.got_ref, f32[2,512,1]{2,1,0:T(8,128)S(1)} %copy-done.12, bf16[16,2,32,256]{3,2,1,0:T(8,128)(2,1)S(1)} %get-tuple-element.69.g_own_ref.own_ref, ...), custom_call_target="tpu_custom_call" | custom-call | flops 805306368 | bytes 4194304 | tf_op jit(solution)/shard_map/mixed/expert_out_kernel/pallas_call | solution.py:95
  147.9 1.2 reduce.1
  149.3 1.2 select_reduce_fusion.1
  151.5 1.1 fusion.1
  152.6 10.1 %all-to-all-done.3 = bf16[8,2,64,768]{3,2,1,0:T(8,128)(2,1)} async-done(((bf16[8,2,64,768]{3,2,1,0:T(8,128)(2,1)}), bf16[8,2,64,768]{3,2,1,0:T(8,128)(2,1)}, u32[]{:S(2)}, u32[]{:S(2)}) %all-to-all-start.3) | async-done | bytes 1572896 | tf_op jit(solution)/shard_map/hidden_grad/all_to_all | solution.py:248
  162.7 1.7 convert_reduce_fusion.1
  164.7 1.9 broadcast_in_dim.97
  166.6 3.6 %all-to-all-start.4 = ((bf16[8,2,64,1536]{3,2,1,0:T(8,128)(2,1)}), bf16[8,2,64,1536]{3,2,1,0:T(8,128)(2,1)S(1)}, u32[]{:S(2)}, u32[]{:S(2)}) async-start(bf16[8,2,64,1536]{3,2,1,0:T(8,128)(2,1)} %broadcast_in_dim.97), calls=%async_computation.4 | async-start | bytes 6291456 | tf_op jit(solution)/shard_map/local_grads/all_to_all | solution.py:157
  170.3 2.1 dynamic-slice_bitcast_fusion
  172.5 2.0 collective-permute-start.14
  174.6 2.1 collective-permute-start.15
  176.7 3.0 %collective-permute-start.16 = (bf16[2,136,256]{2,1,0:T(8,128)(2,1)S(1)}, bf16[2,136,256]{2,1,0:T(8,128)(2,1)S(1)}, u32[]{:S(2)}, u32[]{:S(2)}) collective-permute-start(bf16[2,136,256]{2,1,0:T(8,128)(2,1)S(1)} %get-tuple-element.63), channel_id=1, source_target_pairs={{0,8},{1,9},{2,10},{3,11},{4,12},{5,13},{6,14},{7,15},{8,0},{9,1},... | collective-permute-start | bytes 417800 | tf_op jit(solution)/shard_map/mixed/ppermute | solution.py:182
  179.7 1.5 collective-permute-start.17
  181.2 1.3 collective-permute-done.13.refs_1_
  182.5 2.3 collective-permute-start.18
  185.0 8.6 %collective-permute-start.19 = (bf16[2,136,256]{2,1,0:T(8,128)(2,1)S(1)}, bf16[2,136,256]{2,1,0:T(8,128)(2,1)S(1)}, u32[]{:S(2)}, u32[]{:S(2)}) collective-permute-start(bf16[2,136,256]{2,1,0:T(8,128)(2,1)S(1)} %get-tuple-element.60), channel_id=1, source_target_pairs={{0,14},{1,15},{2,0},{3,1},{4,2},{5,3},{6,4},{7,5},{8,6},{9,7},{10,... | collective-permute-start | bytes 417800 | tf_op jit(solution)/shard_map/mixed/ppermute | solution.py:182
  193.6 2.2 convolution_convert_fusion.1
  196.7 4.4 %collective-permute-done.18.refs_6_ = bf16[2,136,256]{2,1,0:T(8,128)(2,1)S(1)} collective-permute-done((bf16[2,136,256]{2,1,0:T(8,128)(2,1)S(1)}, bf16[2,136,256]{2,1,0:T(8,128)(2,1)S(1)}, u32[]{:S(2)}, u32[]{:S(2)}) %collective-permute-start.18) | collective-permute-done | bytes 139296 | tf_op jit(solution)/shard_map/mixed/ppermute | solution.py:182
  201.1 3.0 %collective-permute-done.19.refs_7_ = bf16[2,136,256]{2,1,0:T(8,128)(2,1)S(1)} collective-permute-done((bf16[2,136,256]{2,1,0:T(8,128)(2,1)S(1)}, bf16[2,136,256]{2,1,0:T(8,128)(2,1)S(1)}, u32[]{:S(2)}, u32[]{:S(2)}) %collective-permute-start.19) | collective-permute-done | bytes 139296 | tf_op jit(solution)/shard_map/mixed/ppermute | solution.py:182
  204.7 2.1 merge.1
  206.9 1.3 collective-permute-start.20
  208.1 3.6 %collective-permute-done.20 = bf16[192,256]{1,0:T(8,128)(2,1)S(1)} collective-permute-done((bf16[192,256]{1,0:T(8,128)(2,1)}, bf16[192,256]{1,0:T(8,128)(2,1)S(1)}, u32[]{:S(2)}, u32[]{:S(2)}) %collective-permute-start.20) | collective-permute-done | bytes 98336 | tf_op jit(solution)/shard_map/mixed/ppermute | solution.py:319
  211.7 2.5 all-to-all-done.4.got_ref
  214.2 1.4 copy-done.3
  215.6 4.0 %slot_grad_kernel.1 = (bf16[16,2,32,256]{3,2,1,0:T(8,128)(2,1)S(1)}, bf16[16,2,32,256]{3,2,1,0:T(8,128)(2,1)}) custom-call(bf16[8,2,64,1536]{3,2,1,0:T(8,128)(2,1)S(1)} %all-to-all-done.4.got_ref, bf16[2,256,1536]{2,1,0:T(8,128)(2,1)S(1)} %copy-done.3, bf16[2,256,1536]{2,1,0:T(8,128)(2,1)} %collective-permute-done.3.w_other_ref), custom_call_target="tpu_custom_call" | custom-call | flops 1610612736 | bytes 7340032 | tf_op jit(solution)/shard_map/grad_tokens/slot_grad_kernel/pallas_call | solution.py:95
  220.7 2.0 collective-permute-done.21
  222.7 1.5 fusion.34
  224.2 1.5 add_convert_fusion
  225.7 6.1 %all-to-all-start.5 = ((bf16[16,128,256]{2,1,0:T(8,128)(2,1)}), bf16[16,128,256]{2,1,0:T(8,128)(2,1)}, u32[]{:S(2)}, u32[]{:S(2)}) async-start(bf16[16,128,256]{2,1,0:T(8,128)(2,1)} %add_convert_fusion), calls=%async_computation.5 | async-start | bytes 2097152 | tf_op jit(solution)/shard_map/grad_tokens/all_to_all | solution.py:335
  233.1 1.8 convolution_convert_fusion
  237.0 1.7 collective-permute-done.22
  238.6 1.2 broadcast.126.clone.1
  240.8 2.9 %collective-permute-done.23 = f32[8,128]{1,0:T(8,128)S(1)} collective-permute-done((f32[8,128]{1,0:T(8,128)S(1)}, f32[8,128]{1,0:T(8,128)S(1)}, u32[]{:S(2)}, u32[]{:S(2)}) %collective-permute-start.23) | collective-permute-done | bytes 4128 | tf_op jit(solution)/shard_map/grad_gate/ppermute | solution.py:350
  243.9 3.4 %collective-permute-done.24 = f32[8,128]{1,0:T(8,128)S(1)} collective-permute-done((f32[8,128]{1,0:T(8,128)S(1)}, f32[8,128]{1,0:T(8,128)S(1)}, u32[]{:S(2)}, u32[]{:S(2)}) %collective-permute-start.24) | collective-permute-done | bytes 4128 | tf_op jit(solution)/shard_map/grad_gate/ppermute | solution.py:350
  248.3 4.2 %collective-permute-done.25 = f32[8,128]{1,0:T(8,128)S(1)} collective-permute-done((f32[8,128]{1,0:T(8,128)S(1)}, f32[8,128]{1,0:T(8,128)S(1)}, u32[]{:S(2)}, u32[]{:S(2)}) %collective-permute-start.25) | collective-permute-done | bytes 4128 | tf_op jit(solution)/shard_map/grad_gate/ppermute | solution.py:350
  253.2 1.2 slice_dynamic-update-slice_fusion
  254.5 5.4 %all-to-all-done.5 = bf16[16,128,256]{2,1,0:T(8,128)(2,1)} async-done(((bf16[16,128,256]{2,1,0:T(8,128)(2,1)}), bf16[16,128,256]{2,1,0:T(8,128)(2,1)}, u32[]{:S(2)}, u32[]{:S(2)}) %all-to-all-start.5) | async-done | bytes 1048608 | tf_op jit(solution)/shard_map/grad_tokens/all_to_all | solution.py:335
  260.0 2.0 reduce_sum.81
  (190 shorter events, 27.3 us)
Async XLA Ops:
  2.2 11.0 %copy-start.21 = (bf16[4,768,256]{2,1,0:T(8,128)(2,1)S(1)}, bf16[4,768,256]{2,1,0:T(8,128)(2,1)}, u32[]{:S(2)}) copy-start(bf16[4,768,256]{2,1,0:T(8,128)(2,1)} %param.12) | copy-start | bytes 4718596
  3.2 38.8 %all-to-all-start = ((bf16[16,136,256]{2,1,0:T(8,128)(2,1)}), bf16[16,136,256]{2,1,0:T(8,128)(2,1)}, u32[]{:S(2)}, u32[]{:S(2)}) async-start(bf16[16,136,256]{2,1,0:T(8,128)(2,1)} %broadcast_in_dim.88), calls=%async_computation | async-start | bytes 2228224 | tf_op jit(solution)/shard_map/send_tokens/all_to_all | solution.py:157
  13.2 1.7 copy-start.22
  14.2 1.5 copy-start.23
  14.2 8.2 %collective-permute-start.1 = (bf16[2,768,256]{2,1,0:T(8,128)(2,1)}, bf16[2,768,256]{2,1,0:T(8,128)(2,1)}, u32[]{:S(2)}, u32[]{:S(2)}) collective-permute-start(bf16[2,768,256]{2,1,0:T(8,128)(2,1)} %get-tuple-element.55), channel_id=1, source_target_pairs={{0,16},{16,0},{32,48},{48,32},{64,80},{80,64},{96,112},{112,96},{1... | collective-permute-start | bytes 2359304 | tf_op jit(solution)/shard_map/swap_weights/ppermute | solution.py:185
  15.8 1.4 copy-start.40
  15.9 1.4 copy-start.28
  17.2 30.0 %copy-start.2 = (bf16[2,256,1536]{2,1,0:T(8,128)(2,1)}, bf16[2,256,1536]{2,1,0:T(8,128)(2,1)S(1)}, u32[]{:S(2)}) copy-start(bf16[2,256,1536]{2,1,0:T(8,128)(2,1)S(1)} %get-tuple-element.49.w_own_ref) | copy-start | bytes 4718596
  17.2 28.1 %collective-permute-start.3 = (bf16[2,256,1536]{2,1,0:T(8,128)(2,1)}, bf16[2,256,1536]{2,1,0:T(8,128)(2,1)}, u32[]{:S(2)}, u32[]{:S(2)}) collective-permute-start(bf16[2,256,1536]{2,1,0:T(8,128)(2,1)} %get-tuple-element.48), channel_id=1, source_target_pairs={{0,16},{16,0},{32,48},{48,32},{64,80},{80,64},{96,112},{112,96},{1... | collective-permute-start | bytes 4718600 | tf_op jit(solution)/shard_map/swap_weights/ppermute | solution.py:185
  17.3 5.1 %collective-permute-start = (bf16[144,256]{1,0:T(8,128)(2,1)S(1)}, bf16[144,256]{1,0:T(8,128)(2,1)S(1)}, u32[]{:S(2)}, u32[]{:S(2)}) collective-permute-start(bf16[144,256]{1,0:T(8,128)(2,1)S(1)} %maximum_maximum_fusion), channel_id=1, source_target_pairs={{0,1},{1,0},{2,3},{3,2},{4,5},{5,4},{6,7},{7,6},{8,9},{9,8},{10,11... | collective-permute-start | bytes 221192 | tf_op jit(solution)/shard_map/send_grads/ppermute | solution.py:208
  22.4 22.8 %copy-start.37 = (bf16[144,256]{1,0:T(8,128)(2,1)}, bf16[144,256]{1,0:T(8,128)(2,1)S(1)}, u32[]{:S(2)}) copy-start(bf16[144,256]{1,0:T(8,128)(2,1)S(1)} %collective-permute-done) | copy-start | bytes 221188
  45.2 2.0 collective-permute-start.2
  47.2 5.2 %copy-start.10 = (bf16[16,2,32,256]{3,2,1,0:T(8,128)(2,1)}, bf16[16,2,32,256]{3,2,1,0:T(8,128)(2,1)S(1)}, u32[]{:S(2)}) copy-start(bf16[16,2,32,256]{3,2,1,0:T(8,128)(2,1)S(1)} %collective-permute-done.2.other_ref) | copy-start | bytes 1572868
  53.2 6.2 %copy-start.38 = (bf16[144,256]{1,0:T(8,128)(2,1)S(1)}, bf16[144,256]{1,0:T(8,128)(2,1)}, u32[]{:S(2)}) copy-start(bf16[144,256]{1,0:T(8,128)(2,1)} %copy-done.37) | copy-start | bytes 221188
  53.2 52.0 %all-to-all-start.1 = ((bf16[8,2,64,1536]{3,2,1,0:T(8,128)(2,1)}), bf16[8,2,64,1536]{3,2,1,0:T(8,128)(2,1)}, u32[]{:S(2)}, u32[]{:S(2)}) async-start(bf16[8,2,64,1536]{3,2,1,0:T(8,128)(2,1)} %partials.2), calls=%async_computation.1 | async-start | bytes 6291456 | tf_op jit(solution)/shard_map/gate_up/all_to_all | solution.py:248
  59.5 11.9 %collective-permute-start.4 = (bf16[2,144,256]{2,1,0:T(8,128)(2,1)S(1)}, bf16[2,144,256]{2,1,0:T(8,128)(2,1)S(1)}, u32[]{:S(2)}, u32[]{:S(2)}) collective-permute-start(bf16[2,144,256]{2,1,0:T(8,128)(2,1)S(1)} %pad_maximum_fusion.1), channel_id=1, source_target_pairs={{0,2},{1,3},{2,4},{3,5},{4,6},{5,7},{6,8},{7,9},{8,10},{9,11},{10,... | collective-permute-start | bytes 442376 | tf_op jit(solution)/shard_map/all_grads/ppermute | solution.py:182
  59.8 12.5 %collective-permute-start.5 = (bf16[2,144,256]{2,1,0:T(8,128)(2,1)S(1)}, bf16[2,144,256]{2,1,0:T(8,128)(2,1)S(1)}, u32[]{:S(2)}, u32[]{:S(2)}) collective-permute-start(bf16[2,144,256]{2,1,0:T(8,128)(2,1)S(1)} %pad_maximum_fusion.1), channel_id=1, source_target_pairs={{0,4},{1,5},{2,6},{3,7},{4,8},{5,9},{6,10},{7,11},{8,12},{9,13},{1... | collective-permute-start | bytes 442376 | tf_op jit(solution)/shard_map/all_grads/ppermute | solution.py:182
  61.5 23.6 %collective-permute-start.6 = (bf16[2,144,256]{2,1,0:T(8,128)(2,1)S(1)}, bf16[2,144,256]{2,1,0:T(8,128)(2,1)S(1)}, u32[]{:S(2)}, u32[]{:S(2)}) collective-permute-start(bf16[2,144,256]{2,1,0:T(8,128)(2,1)S(1)} %pad_maximum_fusion.1), channel_id=1, source_target_pairs={{0,6},{1,7},{2,8},{3,9},{4,10},{5,11},{6,12},{7,13},{8,14},{9,15},... | collective-permute-start | bytes 442376 | tf_op jit(solution)/shard_map/all_grads/ppermute | solution.py:182
  63.6 21.6 %collective-permute-start.7 = (bf16[2,144,256]{2,1,0:T(8,128)(2,1)S(1)}, bf16[2,144,256]{2,1,0:T(8,128)(2,1)S(1)}, u32[]{:S(2)}, u32[]{:S(2)}) collective-permute-start(bf16[2,144,256]{2,1,0:T(8,128)(2,1)S(1)} %pad_maximum_fusion.1), channel_id=1, source_target_pairs={{0,8},{1,9},{2,10},{3,11},{4,12},{5,13},{6,14},{7,15},{8,0},{9,1},... | collective-permute-start | bytes 442376 | tf_op jit(solution)/shard_map/all_grads/ppermute | solution.py:182
  66.5 18.7 %collective-permute-start.8 = (bf16[2,144,256]{2,1,0:T(8,128)(2,1)S(1)}, bf16[2,144,256]{2,1,0:T(8,128)(2,1)S(1)}, u32[]{:S(2)}, u32[]{:S(2)}) collective-permute-start(bf16[2,144,256]{2,1,0:T(8,128)(2,1)S(1)} %pad_maximum_fusion.1), channel_id=1, source_target_pairs={{0,10},{1,11},{2,12},{3,13},{4,14},{5,15},{6,0},{7,1},{8,2},{9,3},... | collective-permute-start | bytes 442376 | tf_op jit(solution)/shard_map/all_grads/ppermute | solution.py:182
  71.3 19.4 %collective-permute-start.9 = (bf16[2,144,256]{2,1,0:T(8,128)(2,1)S(1)}, bf16[2,144,256]{2,1,0:T(8,128)(2,1)S(1)}, u32[]{:S(2)}, u32[]{:S(2)}) collective-permute-start(bf16[2,144,256]{2,1,0:T(8,128)(2,1)S(1)} %pad_maximum_fusion.1), channel_id=1, source_target_pairs={{0,12},{1,13},{2,14},{3,15},{4,0},{5,1},{6,2},{7,3},{8,4},{9,5},{1... | collective-permute-start | bytes 442376 | tf_op jit(solution)/shard_map/all_grads/ppermute | solution.py:182
  72.3 20.6 %collective-permute-start.10 = (bf16[2,144,256]{2,1,0:T(8,128)(2,1)S(1)}, bf16[2,144,256]{2,1,0:T(8,128)(2,1)S(1)}, u32[]{:S(2)}, u32[]{:S(2)}) collective-permute-start(bf16[2,144,256]{2,1,0:T(8,128)(2,1)S(1)} %pad_maximum_fusion.1), channel_id=1, source_target_pairs={{0,14},{1,15},{2,0},{3,1},{4,2},{5,3},{6,4},{7,5},{8,6},{9,7},{10,... | collective-permute-start | bytes 442376 | tf_op jit(solution)/shard_map/all_grads/ppermute | solution.py:182
  110.0 26.7 %all-to-all-start.2 = ((bf16[8,2,64,768]{3,2,1,0:T(8,128)(2,1)}), bf16[8,2,64,768]{3,2,1,0:T(8,128)(2,1)S(1)}, u32[]{:S(2)}, u32[]{:S(2)}) async-start(bf16[8,2,64,768]{3,2,1,0:T(8,128)(2,1)} %broadcast_in_dim.89), calls=%async_computation.2 | async-start | bytes 3145728 | tf_op jit(solution)/shard_map/gate_up/all_to_all | solution.py:157
  117.9 23.1 %copy-start.4 = (bf16[16,2,32,256]{3,2,1,0:T(8,128)(2,1)}, bf16[16,2,32,256]{3,2,1,0:T(8,128)(2,1)S(1)}, u32[]{:S(2)}) copy-start(bf16[16,2,32,256]{3,2,1,0:T(8,128)(2,1)S(1)} %get-tuple-element.69.g_own_ref.own_ref) | copy-start | bytes 1572868
  117.9 2.3 collective-permute-start.11
  120.2 20.8 %copy-start.8 = (bf16[16,2,32,256]{3,2,1,0:T(8,128)(2,1)}, bf16[16,2,32,256]{3,2,1,0:T(8,128)(2,1)S(1)}, u32[]{:S(2)}) copy-start(bf16[16,2,32,256]{3,2,1,0:T(8,128)(2,1)S(1)} %collective-permute-done.11.g_other_ref.other_ref) | copy-start | bytes 1572868
  136.7 4.3 %copy-start = (bf16[8,2,64,768]{3,2,1,0:T(8,128)(2,1)}, bf16[8,2,64,768]{3,2,1,0:T(8,128)(2,1)S(1)}, u32[]{:S(2)}) copy-start(bf16[8,2,64,768]{3,2,1,0:T(8,128)(2,1)S(1)} %all-to-all-done.2.got_ref) | copy-start | bytes 4718596
  136.7 26.0 %all-to-all-start.3 = ((bf16[8,2,64,768]{3,2,1,0:T(8,128)(2,1)}), bf16[8,2,64,768]{3,2,1,0:T(8,128)(2,1)}, u32[]{:S(2)}, u32[]{:S(2)}) async-start(bf16[8,2,64,768]{3,2,1,0:T(8,128)(2,1)} %partials.3), calls=%async_computation.3 | async-start | bytes 3145728 | tf_op jit(solution)/shard_map/hidden_grad/all_to_all | solution.py:248
  141.1 1.0 copy-start.12
  147.9 2.6 collective-permute-start.12
  149.2 1.8 copy-start.15
  151.5 12.9 %copy-start.19 = (f32[2,64,1536]{2,1,0:T(8,128)S(1)}, f32[2,64,1536]{2,1,0:T(8,128)}, u32[]{:S(2)}) copy-start(f32[2,64,1536]{2,1,0:T(8,128)} %copy-done.18) | copy-start | bytes 2359300
  166.6 47.6 %all-to-all-start.4 = ((bf16[8,2,64,1536]{3,2,1,0:T(8,128)(2,1)}), bf16[8,2,64,1536]{3,2,1,0:T(8,128)(2,1)S(1)}, u32[]{:S(2)}, u32[]{:S(2)}) async-start(bf16[8,2,64,1536]{3,2,1,0:T(8,128)(2,1)} %broadcast_in_dim.97), calls=%async_computation.4 | async-start | bytes 6291456 | tf_op jit(solution)/shard_map/local_grads/all_to_all | solution.py:157
  170.3 4.1 %copy-start.5 = (bf16[16,2,32,256]{3,2,1,0:T(8,128)(2,1)S(1)}, bf16[16,2,32,256]{3,2,1,0:T(8,128)(2,1)}, u32[]{:S(2)}) copy-start(bf16[16,2,32,256]{3,2,1,0:T(8,128)(2,1)} %copy-done.4) | copy-start | bytes 1572868
  170.3 4.1 %copy-start.9 = (bf16[16,2,32,256]{3,2,1,0:T(8,128)(2,1)S(1)}, bf16[16,2,32,256]{3,2,1,0:T(8,128)(2,1)}, u32[]{:S(2)}) copy-start(bf16[16,2,32,256]{3,2,1,0:T(8,128)(2,1)} %copy-done.8) | copy-start | bytes 1572868
  172.5 10.0 %collective-permute-start.13 = (bf16[2,136,256]{2,1,0:T(8,128)(2,1)S(1)}, bf16[2,136,256]{2,1,0:T(8,128)(2,1)S(1)}, u32[]{:S(2)}, u32[]{:S(2)}) collective-permute-start(bf16[2,136,256]{2,1,0:T(8,128)(2,1)S(1)} %get-tuple-element.66), channel_id=1, source_target_pairs={{0,2},{1,3},{2,4},{3,5},{4,6},{5,7},{6,8},{7,9},{8,10},{9,11},{10,... | collective-permute-start | bytes 417800 | tf_op jit(solution)/shard_map/mixed/ppermute | solution.py:182
  172.5 12.5 %collective-permute-start.14 = (bf16[2,136,256]{2,1,0:T(8,128)(2,1)S(1)}, bf16[2,136,256]{2,1,0:T(8,128)(2,1)S(1)}, u32[]{:S(2)}, u32[]{:S(2)}) collective-permute-start(bf16[2,136,256]{2,1,0:T(8,128)(2,1)S(1)} %get-tuple-element.65), channel_id=1, source_target_pairs={{0,4},{1,5},{2,6},{3,7},{4,8},{5,9},{6,10},{7,11},{8,12},{9,13},{1... | collective-permute-start | bytes 417800 | tf_op jit(solution)/shard_map/mixed/ppermute | solution.py:182
  174.5 10.2 %copy-start.1 = (bf16[8,2,64,768]{3,2,1,0:T(8,128)(2,1)S(1)}, bf16[8,2,64,768]{3,2,1,0:T(8,128)(2,1)}, u32[]{:S(2)}) copy-start(bf16[8,2,64,768]{3,2,1,0:T(8,128)(2,1)} %copy-done) | copy-start | bytes 4718596
  174.6 21.1 %collective-permute-start.15 = (bf16[2,136,256]{2,1,0:T(8,128)(2,1)S(1)}, bf16[2,136,256]{2,1,0:T(8,128)(2,1)S(1)}, u32[]{:S(2)}, u32[]{:S(2)}) collective-permute-start(bf16[2,136,256]{2,1,0:T(8,128)(2,1)S(1)} %get-tuple-element.64), channel_id=1, source_target_pairs={{0,6},{1,7},{2,8},{3,9},{4,10},{5,11},{6,12},{7,13},{8,14},{9,15},... | collective-permute-start | bytes 417800 | tf_op jit(solution)/shard_map/mixed/ppermute | solution.py:182
  176.7 19.0 %collective-permute-start.16 = (bf16[2,136,256]{2,1,0:T(8,128)(2,1)S(1)}, bf16[2,136,256]{2,1,0:T(8,128)(2,1)S(1)}, u32[]{:S(2)}, u32[]{:S(2)}) collective-permute-start(bf16[2,136,256]{2,1,0:T(8,128)(2,1)S(1)} %get-tuple-element.63), channel_id=1, source_target_pairs={{0,8},{1,9},{2,10},{3,11},{4,12},{5,13},{6,14},{7,15},{8,0},{9,1},... | collective-permute-start | bytes 417800 | tf_op jit(solution)/shard_map/mixed/ppermute | solution.py:182
  179.7 17.0 %collective-permute-start.17 = (bf16[2,136,256]{2,1,0:T(8,128)(2,1)S(1)}, bf16[2,136,256]{2,1,0:T(8,128)(2,1)S(1)}, u32[]{:S(2)}, u32[]{:S(2)}) collective-permute-start(bf16[2,136,256]{2,1,0:T(8,128)(2,1)S(1)} %get-tuple-element.62), channel_id=1, source_target_pairs={{0,10},{1,11},{2,12},{3,13},{4,14},{5,15},{6,0},{7,1},{8,2},{9,3},... | collective-permute-start | bytes 417800 | tf_op jit(solution)/shard_map/mixed/ppermute | solution.py:182
  182.5 2.3 copy-start.29
  182.5 18.5 %collective-permute-start.18 = (bf16[2,136,256]{2,1,0:T(8,128)(2,1)S(1)}, bf16[2,136,256]{2,1,0:T(8,128)(2,1)S(1)}, u32[]{:S(2)}, u32[]{:S(2)}) collective-permute-start(bf16[2,136,256]{2,1,0:T(8,128)(2,1)S(1)} %get-tuple-element.61), channel_id=1, source_target_pairs={{0,12},{1,13},{2,14},{3,15},{4,0},{5,1},{6,2},{7,3},{8,4},{9,5},{1... | collective-permute-start | bytes 417800 | tf_op jit(solution)/shard_map/mixed/ppermute | solution.py:182
  185.0 8.6 %copy-start.30 = (bf16[2,136,256]{2,1,0:T(8,128)(2,1)}, bf16[2,136,256]{2,1,0:T(8,128)(2,1)S(1)}, u32[]{:S(2)}) copy-start(bf16[2,136,256]{2,1,0:T(8,128)(2,1)S(1)} %collective-permute-done.14.refs_2_) | copy-start | bytes 417796
  185.0 19.1 %collective-permute-start.19 = (bf16[2,136,256]{2,1,0:T(8,128)(2,1)S(1)}, bf16[2,136,256]{2,1,0:T(8,128)(2,1)S(1)}, u32[]{:S(2)}, u32[]{:S(2)}) collective-permute-start(bf16[2,136,256]{2,1,0:T(8,128)(2,1)S(1)} %get-tuple-element.60), channel_id=1, source_target_pairs={{0,14},{1,15},{2,0},{3,1},{4,2},{5,3},{6,4},{7,5},{8,6},{9,7},{10,... | collective-permute-start | bytes 417800 | tf_op jit(solution)/shard_map/mixed/ppermute | solution.py:182
  195.7 8.3 %copy-start.31 = (bf16[2,136,256]{2,1,0:T(8,128)(2,1)}, bf16[2,136,256]{2,1,0:T(8,128)(2,1)S(1)}, u32[]{:S(2)}) copy-start(bf16[2,136,256]{2,1,0:T(8,128)(2,1)S(1)} %collective-permute-done.15.refs_3_) | copy-start | bytes 417796
  195.8 8.3 %copy-start.32 = (bf16[2,136,256]{2,1,0:T(8,128)(2,1)}, bf16[2,136,256]{2,1,0:T(8,128)(2,1)S(1)}, u32[]{:S(2)}) copy-start(bf16[2,136,256]{2,1,0:T(8,128)(2,1)S(1)} %collective-permute-done.16.refs_4_) | copy-start | bytes 417796
  196.7 7.4 %copy-start.33 = (bf16[2,136,256]{2,1,0:T(8,128)(2,1)}, bf16[2,136,256]{2,1,0:T(8,128)(2,1)S(1)}, u32[]{:S(2)}) copy-start(bf16[2,136,256]{2,1,0:T(8,128)(2,1)S(1)} %collective-permute-done.17.refs_5_) | copy-start | bytes 417796
  201.0 3.0 %copy-start.34 = (bf16[2,136,256]{2,1,0:T(8,128)(2,1)}, bf16[2,136,256]{2,1,0:T(8,128)(2,1)S(1)}, u32[]{:S(2)}) copy-start(bf16[2,136,256]{2,1,0:T(8,128)(2,1)S(1)} %collective-permute-done.18.refs_6_) | copy-start | bytes 417796
  206.9 4.8 %collective-permute-start.20 = (bf16[192,256]{1,0:T(8,128)(2,1)}, bf16[192,256]{1,0:T(8,128)(2,1)S(1)}, u32[]{:S(2)}, u32[]{:S(2)}) collective-permute-start(bf16[192,256]{1,0:T(8,128)(2,1)} %get-tuple-element.34), channel_id=1, source_target_pairs={{0,1},{1,0},{2,3},{3,2},{4,5},{5,4},{6,7},{7,6},{8,9},{9,8},{10,11... | collective-permute-start | bytes 294920 | tf_op jit(solution)/shard_map/mixed/ppermute | solution.py:319
  214.2 1.4 copy-start.3
  220.4 2.3 collective-permute-start.21
  220.7 3.5 %copy-start.17 = (bf16[16,2,32,256]{3,2,1,0:T(8,128)(2,1)S(1)}, bf16[16,2,32,256]{3,2,1,0:T(8,128)(2,1)}, u32[]{:S(2)}) copy-start(bf16[16,2,32,256]{3,2,1,0:T(8,128)(2,1)} %copy-done.16) | copy-start | bytes 1572868
  225.7 34.3 %all-to-all-start.5 = ((bf16[16,128,256]{2,1,0:T(8,128)(2,1)}), bf16[16,128,256]{2,1,0:T(8,128)(2,1)}, u32[]{:S(2)}, u32[]{:S(2)}) async-start(bf16[16,128,256]{2,1,0:T(8,128)(2,1)} %add_convert_fusion), calls=%async_computation.5 | async-start | bytes 2097152 | tf_op jit(solution)/shard_map/grad_tokens/all_to_all | solution.py:335
  231.8 1.2 copy-start.11
  235.1 1.4 copy-start.26
  235.1 18.0 %collective-permute-start.26 = (bf16[2,256,1536]{2,1,0:T(8,128)(2,1)S(1)}, bf16[2,256,1536]{2,1,0:T(8,128)(2,1)S(1)}, u32[]{:S(2)}, u32[]{:S(2)}) collective-permute-start(bf16[2,256,1536]{2,1,0:T(8,128)(2,1)S(1)} %slice.138), channel_id=1, source_target_pairs={{0,16},{16,0},{32,48},{48,32},{64,80},{80,64},{96,112},{112,96},{1... | collective-permute-start | bytes 4718600 | tf_op jit(solution)/shard_map/weight_grads/ppermute | solution.py:185
  236.0 2.6 collective-permute-start.22
  236.6 16.4 %collective-permute-start.27 = (bf16[2,768,256]{2,1,0:T(8,128)(2,1)S(1)}, bf16[2,768,256]{2,1,0:T(8,128)(2,1)S(1)}, u32[]{:S(2)}, u32[]{:S(2)}) collective-permute-start(bf16[2,768,256]{2,1,0:T(8,128)(2,1)S(1)} %get-tuple-element.50), channel_id=1, source_target_pairs={{0,16},{16,0},{32,48},{48,32},{64,80},{80,64},{96,112},{112,96},{1... | collective-permute-start | bytes 2359304 | tf_op jit(solution)/shard_map/weight_grads/ppermute | solution.py:185
  238.6 5.1 %collective-permute-start.23 = (f32[8,128]{1,0:T(8,128)S(1)}, f32[8,128]{1,0:T(8,128)S(1)}, u32[]{:S(2)}, u32[]{:S(2)}) collective-permute-start(f32[8,128]{1,0:T(8,128)S(1)} %add.317), channel_id=1, source_target_pairs={{0,32},{16,48},{32,0},{48,16},{64,96},{80,112},{96,64},{112,80},{1... | collective-permute-start | bytes 12296 | tf_op jit(solution)/shard_map/grad_gate/ppermute | solution.py:350
  243.8 3.6 %collective-permute-start.24 = (f32[8,128]{1,0:T(8,128)S(1)}, f32[8,128]{1,0:T(8,128)S(1)}, u32[]{:S(2)}, u32[]{:S(2)}) collective-permute-start(f32[8,128]{1,0:T(8,128)S(1)} %add.318), channel_id=1, source_target_pairs={{0,64},{16,80},{32,96},{48,112},{64,0},{80,16},{96,32},{112,48},{1... | collective-permute-start | bytes 12296 | tf_op jit(solution)/shard_map/grad_gate/ppermute | solution.py:350
  247.4 5.1 %collective-permute-start.25 = (f32[8,128]{1,0:T(8,128)S(1)}, f32[8,128]{1,0:T(8,128)S(1)}, u32[]{:S(2)}, u32[]{:S(2)}) collective-permute-start(f32[8,128]{1,0:T(8,128)S(1)} %add.319), channel_id=1, source_target_pairs={{0,128},{16,144},{32,160},{48,176},{64,192},{80,208},{96,224},{112... | collective-permute-start | bytes 12296 | tf_op jit(solution)/shard_map/grad_gate/ppermute | solution.py:350
  253.1 1.4 copy-start.24
  254.5 7.4 %copy-start.25 = (bf16[4,256,768]{2,1,0:T(8,128)(2,1)}, bf16[4,256,768]{2,1,0:T(8,128)(2,1)S(1)}, u32[]{:S(2)}) copy-start(bf16[4,256,768]{2,1,0:T(8,128)(2,1)S(1)} %get-tuple-element.52) | copy-start | bytes 4718596
  (11 other events, 9.4 us)
